TPU v7x, 32 devices: a whole 2x2x4 slice. The times are simulated.
32 devices in a mesh: grp: 4 (over x, core), tok: 8 (over z, y).
Axes of the slice: x: 2, y: 2, z: 4, core: 2. Of those that a mesh axis runs over, the one named last changes fastest.
Arguments:
- layer_input: bfloat16 [32768, 768], P(('grp', 'tok')), may hold values from -6 to 6
- doc_starts: int32 [32768], P(('grp', 'tok')), may hold values 0 or 1
- ln1_gain: float32 [768], replicated, may hold values from 0.5 to 1.5
- ln1_shift: float32 [768], replicated, may hold values from -3 to 3
- w_qkv: bfloat16 [768, 2304], replicated, may hold values from -0.21875 to 0.21875
- feat_q: bfloat16 [768, 64], replicated, may hold values from -0.75 to 0.75
- feat_k: bfloat16 [768, 64], replicated, may hold values from -0.75 to 0.75
- w_out: bfloat16 [768, 768], replicated, may hold values from -6 to 6
- ln2_gain: float32 [768], replicated, may hold values from 0.5 to 1.5
- ln2_shift: float32 [768], replicated, may hold values from -3 to 3
- w_fc: bfloat16 [768, 3072], replicated, may hold values from -0.21875 to 0.21875
- w_proj: bfloat16 [3072, 768], replicated, may hold values from -0.109375 to 0.109375
- cotangent: bfloat16 [32768, 768], P(('grp', 'tok')), may hold values from -6 to 6
Outputs:
- output: bfloat16 [32768, 768], P(('grp', 'tok'))
- grad_input: float32 [32768, 768], P(('grp', 'tok'))
- grad_ln1_gain: float32 [768], P('tok')
- grad_ln1_shift: float32 [768], P('tok')
- grad_qkv: float32 [768, 2304], P('tok')
- grad_feat_q: float32 [768, 64], P('tok')
- grad_feat_k: float32 [768, 64], P('tok')
- grad_w_out: float32 [768, 768], P('tok')
- grad_ln2_gain: float32 [768], P('tok')
- grad_ln2_shift: float32 [768], P('tok')
- grad_fc: float32 [768, 3072], P('tok')
- grad_proj: float32 [3072, 768], P('tok')
Inputs may be any that keep to these rules, and one draw needn't show every extreme that they name: `doc_starts`: 1 marks the first token of a document; attention and carried sums stop there.
All inputs are finite; a program needn't handle non-finite values. No bound on the sum of `doc_starts` on one device may be relied on, other than what follows from the above.
Results may differ from a plain program's by a relative error of at most 0.011.
Values sent between devices are 32-bit elements; how exact they have to be, the bound alone decides.
No kernel may reach another device: no remote copies, remote signals or barrier semaphores. Data moves between devices by JAX's collectives and lax.ppermute only.
A program may use at most 768 MiB of HBM per device.

v0:
```python
from functools import partial

import jax
import jax.numpy as jnp
from jax import lax
from jax.experimental import pallas as pl
from jax.experimental.pallas import tpu as pltpu
from jax.sharding import PartitionSpec as P


eps = 1e-05
f32 = jnp.float32
bf16 = jnp.bfloat16
grant = 56 * 1024 * 1024


def dg(left, right, left_dim, right_dim):
    dims = (((left_dim,), (right_dim,)), ((), ()))
    return lax.dot_general(left, right, dims, preferred_element_type=f32)


def parts_of(value):
    high = value.astype(bf16).astype(f32)
    return high, value - high


def rows_of(rows, width):
    at = lax.broadcasted_iota(jnp.int32, (16, width), 0)
    block = jnp.zeros((16, width), f32)
    for place, row in enumerate(rows):
        block = jnp.where(at == place, row, block)
    return block


def stacked(*blocks):
    return jnp.concatenate([block.astype(bf16) for block in blocks], axis=0)


def norm_parts(value):
    centered = value - jnp.mean(value, axis=1, keepdims=True)
    variance = jnp.mean(centered * centered, axis=1, keepdims=True)
    scale = lax.rsqrt(variance + eps)
    return centered * scale, scale


def norm_back(unit, scale, gain, grad):
    scaled = grad * gain
    along = jnp.mean(scaled * unit, axis=1, keepdims=True)
    return scale * (scaled - jnp.mean(scaled, axis=1, keepdims=True) - unit * along)


def enter_kernel(
    x_ref, gain_ref, shift_ref, w_ref, fq_ref, fk_ref, tail_ref,
    hid_ref, qkv_ref, pq_ref, pk_ref, state_ref, norm_ref,
):
    width, head_dim = fq_ref.shape
    rows = x_ref.shape[0]
    unit, _ = norm_parts(x_ref[...].astype(f32))
    hid = (unit * gain_ref[...] + shift_ref[...]).astype(bf16)
    hid_ref[...] = hid
    qkv_ref[...] = dg(w_ref[...], hid, 0, 1).astype(bf16)

    @pl.when(pl.program_id(0) == 0)
    def _():
        state_ref[...] = jnp.zeros_like(state_ref)
        norm_ref[...] = jnp.zeros_like(norm_ref)

    def features(maps, token_rows):
        logits = dg(maps, token_rows, 0, 0)
        up = jnp.exp(logits - jnp.max(logits, axis=0, keepdims=True))
        down = jnp.exp(jnp.min(logits, axis=0, keepdims=True) - logits)
        up = up / jnp.sum(up, axis=0, keepdims=True)
        down = down / jnp.sum(down, axis=0, keepdims=True)
        return stacked(up, down)

    ones = jnp.ones((16, rows), bf16)
    for head in range(width // head_dim):
        low, high = (head * head_dim, (head + 1) * head_dim)
        pq_ref[2 * low : 2 * high, :] = features(fq_ref[low:high, :], qkv_ref[low:high, :])
        phi = features(fk_ref[low:high, :], qkv_ref[width + low : width + high, :])
        pk_ref[2 * low : 2 * high, :] = phi
        wide = stacked(qkv_ref[2 * width + low : 2 * width + high, :], ones)
        local = dg(wide, phi * tail_ref[...], 1, 1)
        state_ref[low:high, :] += local[:head_dim]
        norm_ref[head : head + 1, :] += local[head_dim : head_dim + 1]


def masked(scores, start, offset):
    key_at = lax.broadcasted_iota(jnp.int32, scores.shape, 0)
    query_at = lax.broadcasted_iota(jnp.int32, scores.shape, 1) + offset
    allowed = (key_at >= start) & (key_at <= query_at)
    return jnp.where(allowed, scores, 0.0).astype(bf16)


def local_kernel(pq_ref, pk_ref, v_ref, start_ref, num_ref, den_ref):
    tokens = pq_ref.shape[1]
    head_dim = v_ref.shape[0]
    step = min(256, tokens)
    for low in range(0, tokens, step):
        high = low + step
        scores = dg(pk_ref[:, :high], pq_ref[:, low:high], 0, 0)
        weights = masked(scores, start_ref[:, low:high], low)
        wide = stacked(v_ref[:, :high], jnp.ones((16, high), bf16))
        local = dg(wide, weights, 1, 0)
        num_ref[:, low:high] = local[:head_dim]
        den_ref[0, :, low:high] = local[head_dim : head_dim + 1]


def mix_kernel(
    num0_ref, num1_ref, den0_ref, den1_ref, pq_ref, state_ref, norm_ref, open_ref, x_ref, wout_ref, gain_ref, shift_ref, wfc_ref,
    mixed_ref, low_ref, denom_ref, resid_ref, hid_ref, act_ref, slope_ref,
):
    width, features = state_ref.shape
    head_dim = features // 2
    opened = open_ref[...]
    for head in range(width // head_dim):
        low, high = (head * head_dim, (head + 1) * head_dim)
        state = parts_of(state_ref[low:high, :])
        normer = rows_of(parts_of(norm_ref[head : head + 1, :]), features)
        carry = dg(stacked(*state, normer), pq_ref[2 * low : 2 * high, :], 1, 0)
        half = width // 2
        num_ref, den_ref = (num0_ref, den0_ref) if low < half else (num1_ref, den1_ref)
        num = num_ref[low % half : low % half + head_dim, :]
        num = num + opened * (carry[:head_dim] + carry[head_dim:features])
        den = den_ref[head % (half // head_dim)] + opened * (carry[features : features + 1] + carry[features + 1 : features + 2])
        mixed = num / den
        denom_ref[head] = den
        mixed_ref[low:high, :] = mixed
        low_ref[low:high, :] = mixed.astype(bf16)
    resid = x_ref[...].astype(f32) + dg(low_ref[...], wout_ref[...], 0, 0)
    resid_ref[...] = resid
    unit, _ = norm_parts(resid)
    hid = (unit * gain_ref[...] + shift_ref[...]).astype(bf16)
    hid_ref[...] = hid
    hidden = wfc_ref.shape[1]
    step = hidden // 4
    root = 0.7978845608028654
    for low in range(0, hidden, step):
        pre = dg(hid, wfc_ref[:, low : low + step], 1, 0)
        square = pre * pre
        bent = jnp.tanh(root * pre * (1.0 + 0.044715 * square))
        half = 0.5 * (1.0 + bent)
        act_ref[:, low : low + step] = (pre * half).astype(bf16)
        curve = 0.5 * pre * (1.0 - bent * bent) * (root * (1.0 + 0.134145 * square))
        slope_ref[:, low : low + step] = (half + curve).astype(bf16)


def slope_kernel(slope_ref, cot_ref, wproj_ref, dpre_ref):
    hidden = slope_ref.shape[1]
    step = hidden // 4
    for low in range(0, hidden, step):
        dact = dg(cot_ref[...], wproj_ref[low : low + step, :], 1, 1)
        dpre_ref[:, low : low + step] = (dact * slope_ref[:, low : low + step].astype(f32)).astype(bf16)


def out_kernel(act_ref, resid_ref, wproj_ref, out_ref):
    out_ref[...] = (resid_ref[...] + dg(act_ref[...], wproj_ref[...], 1, 0)).astype(bf16)


def back_kernel(
    dpre_ref, resid_ref, cot_ref, wfc_ref, gain_ref, wout_ref, mixed_ref, denom_ref, pq_ref, open_ref,
    dbranch_ref, dresid_ref, dnum_ref, dden_ref, state_ref, norm_ref, sums_ref,
):
    width = mixed_ref.shape[0]
    features = state_ref.shape[1]
    head_dim = features // 2
    rows = dpre_ref.shape[0]

    @pl.when(pl.program_id(0) == 0)
    def _():
        state_ref[...] = jnp.zeros_like(state_ref)
        norm_ref[...] = jnp.zeros_like(norm_ref)
        sums_ref[...] = jnp.zeros_like(sums_ref)

    dhid = dg(dpre_ref[...], wfc_ref[...], 1, 1)
    unit, scale = norm_parts(resid_ref[...])
    sums_ref[0:1, :] += jnp.sum(dhid * unit, axis=0, keepdims=True)
    sums_ref[1:2, :] += jnp.sum(dhid, axis=0, keepdims=True)
    dresid = cot_ref[...].astype(f32) + norm_back(unit, scale, gain_ref[...], dhid)
    dresid_ref[...] = dresid
    dbranch = dresid.astype(bf16)
    dbranch_ref[...] = dbranch
    dmixed_all = dg(wout_ref[...], dbranch, 1, 1)
    opened = open_ref[...]
    for head in range(width // head_dim):
        low, high = (head * head_dim, (head + 1) * head_dim)
        dmixed = dmixed_all[low:high]
        inverse = 1.0 / denom_ref[head]
        dnum = dmixed * inverse
        dden = -jnp.sum(dmixed * mixed_ref[low:high, :], axis=0, keepdims=True) * inverse
        dnum_ref[low:high, :] = dnum
        dden_ref[head] = dden
        wide = stacked(*parts_of(dnum * opened), rows_of(parts_of(dden * opened), rows))
        local = dg(wide, pq_ref[2 * low : 2 * high, :], 1, 1)
        state_ref[low:high, :] += local[:head_dim] + local[head_dim:features]
        norm_ref[head : head + 1, :] += local[features : features + 1] + local[features + 1 : features + 2]


def logit_back(phi, dphi):
    half = phi.shape[0] // 2
    up, down = (phi[:half].astype(f32), phi[half:].astype(f32))
    dup, ddown = (dphi[:half], dphi[half:])
    dup = dup - jnp.sum(dup * up, axis=0, keepdims=True)
    ddown = ddown - jnp.sum(ddown * down, axis=0, keepdims=True)
    return (up * dup - down * ddown).astype(bf16)


def local_back_kernel(
    pq_ref, pk_ref, q_ref, v_ref, dnum_ref, dden_ref, start_ref, open_ref, state_ref, norm_ref, fq_ref,
    dq_ref, gfq_ref, dphik_ref, dv_ref,
):
    tokens = pq_ref.shape[1]
    features = pq_ref.shape[0]
    step = min(256, tokens)
    state_high, state_low = parts_of(state_ref[...])
    norm_high, norm_low = parts_of(norm_ref[0])
    carried = stacked(
        state_high, state_high, state_low, rows_of((norm_high, norm_high, norm_low), features)
    )
    dphik_ref[...] = jnp.zeros_like(dphik_ref)
    dv_ref[...] = jnp.zeros_like(dv_ref)
    maps = fq_ref[...]
    gfq = jnp.zeros(gfq_ref.shape[1:], f32)
    for low in range(0, tokens, step):
        high = low + step
        start = start_ref[:, low:high]
        phi = pq_ref[:, low:high]
        num_high, num_low = parts_of(dnum_ref[:, low:high])
        dnum_low = num_high.astype(bf16)
        dden = dden_ref[0, :, low:high]
        weights = masked(dg(pk_ref[:, :high], phi, 0, 0), start, low)
        dweights = masked(dg(v_ref[:, :high], dnum_low, 0, 0) + dden, start, low)
        dv_ref[:, :high] += dg(dnum_low, weights, 1, 1)
        dphik_ref[:, :high] += dg(phi, dweights, 1, 1)
        den_high, den_low = parts_of(dden)
        arriving = stacked(num_high, num_low, num_high, rows_of((den_high, den_low, den_high), step))
        dphi = dg(pk_ref[:, :high], dweights, 1, 0)
        dphi = dphi + open_ref[:, low:high] * dg(carried, arriving, 0, 0)
        dlogit = logit_back(phi, dphi)
        gfq = gfq + dg(q_ref[:, low:high], dlogit, 1, 1)
        dq_ref[:, low:high] = dg(maps, dlogit, 1, 0).astype(bf16)
    gfq_ref[0] = gfq


def key_back_kernel(
    pk_ref, k_ref, v_ref, dphik0_ref, dphik1_ref, dv0_ref, dv1_ref, tail_ref, state_ref, norm_ref, fk_ref,
    dkv_ref, gfk_ref,
):
    features, tokens = pk_ref.shape
    head_dim = features // 2
    state_high, state_low = parts_of(state_ref[...])
    carried = stacked(state_high, state_low, rows_of(parts_of(norm_ref[0]), features))
    values = v_ref[...]
    tail = tail_ref[...]
    wide = stacked(values, values, jnp.ones((16, tokens), bf16))
    phi = pk_ref[...]
    early = pl.program_id(0) < pl.num_programs(0) // 2
    dphi = jnp.where(early, dphik0_ref[...], dphik1_ref[...]) + tail * dg(carried, wide, 0, 0)
    both = dg(stacked(state_high, state_low), phi, 1, 0)
    dv = jnp.where(early, dv0_ref[...], dv1_ref[...]) + tail * (both[:head_dim] + both[head_dim:])
    dlogit = logit_back(phi, dphi)
    gfk_ref[0] = dg(k_ref[...], dlogit, 1, 1)
    dkv_ref[0] = dg(fk_ref[...], dlogit, 1, 0).astype(bf16)
    dkv_ref[1] = dv.astype(bf16)


def leave_kernel(dq0_ref, dq1_ref, dkv_ref, w_ref, x_ref, gain_ref, dresid_ref, grad_ref, sums_ref):
    width = x_ref.shape[1]

    @pl.when(pl.program_id(0) == 0)
    def _():
        sums_ref[...] = jnp.zeros_like(sums_ref)

    dq = jnp.concatenate([dq0_ref[...], dq1_ref[...]], axis=0)
    dhid = dg(dq, w_ref[:, :width], 0, 1)
    dhid = dhid + dg(dkv_ref[0], w_ref[:, width : 2 * width], 0, 1)
    dhid = dhid + dg(dkv_ref[1], w_ref[:, 2 * width :], 0, 1)
    unit, scale = norm_parts(x_ref[...].astype(f32))
    sums_ref[0:1, :] += jnp.sum(dhid * unit, axis=0, keepdims=True)
    sums_ref[1:2, :] += jnp.sum(dhid, axis=0, keepdims=True)
    grad_ref[...] = dresid_ref[...] + norm_back(unit, scale, gain_ref[...], dhid)


def whole(shape):
    return pl.BlockSpec(shape, lambda i: (0,) * len(shape))


def down(rows, width):
    return pl.BlockSpec((rows, width), lambda i: (i, 0))


def across(rows, width):
    return pl.BlockSpec((rows, width), lambda i: (0, i))


def heads_across(heads, width):
    return pl.BlockSpec((heads, 1, width), lambda i: (0, 0, i))


def one_head(width, first=0):
    return pl.BlockSpec((1, 1, width), lambda i: (first + i, 0, 0))


def head_rows(rows, width, first=0):
    return pl.BlockSpec((rows, width), lambda i: (first + i, 0))


def shape_of(shape, dtype):
    return jax.ShapeDtypeStruct(shape, dtype)


def call(kernel, grid, ins, outs, shapes, args):
    return pl.pallas_call(
        kernel,
        grid=(grid,),
        in_specs=ins,
        out_specs=outs,
        out_shape=shapes,
        compiler_params=pltpu.CompilerParams(
            dimension_semantics=("arbitrary",), vmem_limit_bytes=grant
        ),
    )(*args)


def log2_of(count):
    return count.bit_length() - 1


def sizes():
    return (lax.axis_size("grp"), lax.axis_size("tok"))


def place_of():
    return lax.axis_index("grp") * lax.axis_size("tok") + lax.axis_index("tok")


def flips(first, second):
    grp_size, tok_size = sizes()
    pairs = []
    for place in range(grp_size * tok_size):
        pairs.append((place, place ^ (second if (place // tok_size) % 2 else first)))
    return pairs


def far_flips():
    grp_size, tok_size = sizes()
    return [(2 * tok_size) << bit for bit in range(log2_of(grp_size) - 1)]


def order_of(turn):
    tok_bits = [1 << bit for bit in range(log2_of(lax.axis_size("tok")))]
    near = far_flips() + tok_bits[:-1]
    turn = turn % len(near)
    return near[turn:] + near[:turn] + tok_bits[-1:]


def slots_of(turn):
    grp_size, tok_size = sizes()
    order = order_of(turn)
    slots = []
    for tok in range(tok_size):
        for far in range(grp_size // 2):
            place = far * 2 * tok_size + tok
            bits = [(place // flip) % 2 for flip in order]
            slots.append(sum(bit << (len(bits) - 1 - at) for at, bit in enumerate(bits)))
    return jnp.array(slots, jnp.int32)


def tables_of(turns):
    core = lax.axis_index("grp") % 2
    own = lax.axis_index("tok") * (lax.axis_size("grp") // 2) + lax.axis_index("grp") // 2
    even, odd = (slots_of(turns[0]), slots_of(turns[1]))
    mine = jnp.where(core == 0, even, odd)
    theirs = jnp.where(core == 0, odd, even)
    mine = jnp.concatenate([mine ^ mine[own], core[None].astype(jnp.int32)])
    theirs = jnp.concatenate([theirs ^ theirs[own], (1 - core)[None].astype(jnp.int32)])
    return mine, theirs


def product_kernel(forms, has_tail, has_other, table_ref, *refs):
    count = len(forms)
    ins, refs = (refs[: 2 * count], refs[2 * count :])
    tail_ref, refs = (refs[0], refs[1:]) if has_tail else (None, refs)
    other_ref, refs = (refs[0], refs[1:]) if has_other else (None, refs)
    pieces = table_ref.shape[0] - 1
    piece_rows = refs[0].shape[1]
    at = 0
    blocks = []
    for place, (left_dim, right_dim) in enumerate(forms):
        left, right = (ins[2 * place][...], ins[2 * place + 1][...])
        right = right.reshape(right.shape[-2:])
        value = dg(left, right, left_dim, right_dim)
        blocks.append((at, value))
        at += value.shape[1]
    if has_tail:
        blocks.append((at, tail_ref[0]))
    rows = blocks[0][1].shape[0]
    here = rows // piece_rows
    base = pl.program_id(0) * here
    for piece in range(here):
        slot = table_ref[base + piece]
        span = slice(piece * piece_rows, (piece + 1) * piece_rows)
        for column, value in blocks:
            cut = value[span]
            lanes = slice(column, column + cut.shape[1])
            if not has_other:
                refs[0][slot, :, lanes] = cut
                continue
            cut = cut + other_ref[slot, :, lanes]
            keep_ref, give_ref = refs
            half = pieces // 2

            @pl.when(slot < half)
            def _(cut=cut, lanes=lanes):
                keep_ref[slot, :, lanes] = cut

            @pl.when(slot >= half)
            def _(cut=cut, lanes=lanes):
                give_ref[slot - half, :, lanes] = cut


def products(table, forms, ins, specs, rows, block_rows, columns, tail=None, other=None):
    pieces = table.shape[0] - 1
    piece_rows = rows // pieces
    shape = (pieces, piece_rows, columns)
    whole_spec = lambda dims: pl.BlockSpec(dims, lambda i, t: (0,) * len(dims))
    specs = list(specs)
    ins = list(ins)
    if tail is not None:
        ins.append(tail)
        specs.append(pl.BlockSpec((1, block_rows, tail.shape[2]), lambda i, t: (t[pieces], i, 0)))
    if other is not None:
        ins.append(other)
        specs.append(whole_spec(shape))
        half = (pieces // 2, piece_rows, columns)
        outs = [whole_spec(half), whole_spec(half)]
        shapes = [shape_of(half, f32), shape_of(half, f32)]
    else:
        outs = whole_spec(shape)
        shapes = shape_of(shape, f32)
    return pl.pallas_call(
        partial(product_kernel, forms, tail is not None, other is not None),
        grid_spec=pltpu.PrefetchScalarGridSpec(
            num_scalar_prefetch=1, grid=(rows // block_rows,), in_specs=specs, out_specs=outs
        ),
        out_shape=shapes,
        compiler_params=pltpu.CompilerParams(
            dimension_semantics=("arbitrary",), vmem_limit_bytes=grant
        ),
    )(table, *ins)


def send(value, first, second):
    return lax.ppermute(value, ("grp", "tok"), flips(first, second))


def swap_cores(value):
    tok_size = lax.axis_size("tok")
    return send(value, tok_size, tok_size)


def fold(keep, give, turns):
    orders = (order_of(turns[0]), order_of(turns[1]))
    for even, odd in zip(*orders):
        other = send(give, even, odd)
        half = keep.shape[0] // 2
        if half:
            give = keep[half:] + other[half:]
            keep = keep[:half] + other[:half]
        else:
            keep = keep + other
    for flip in far_flips():
        bit = (place_of() & flip) != 0
        other = send(keep, flip, flip)
        keep = jnp.concatenate(
            [jnp.where(bit, other, keep), jnp.where(bit, keep, other)], axis=0
        )
    keep = keep.reshape(-1, keep.shape[2])
    other = swap_cores(keep)
    core = lax.axis_index("grp") % 2
    return (jnp.where(core == 0, keep, other), jnp.where(core == 0, other, keep))


def chain_kernel(backward, got_ref, out_ref):
    count, rows, lanes = got_ref.shape

    def step(at, so_far):
        block = count - 1 - at if backward else at
        out_ref[block] = so_far
        local = got_ref[block]
        return local + local[rows - 1 :, lanes - 1 :] * so_far

    lax.fori_loop(0, count, step, jnp.zeros((rows, lanes), f32))


def carry_scan(state, norm, keep, backward):
    grp_size, tok_size = sizes()
    count = grp_size * tok_size
    lanes = state.shape[1]
    share = state.shape[0] // count
    spare = norm.size // count
    extra = jnp.concatenate(
        [norm.reshape(count, spare), jnp.zeros((count, lanes - 1 - spare), f32), jnp.full((count, 1), keep)],
        axis=1,
    )
    packed = jnp.concatenate([state.reshape(count, share, lanes), extra[:, None]], axis=1)
    landed = lax.all_to_all(packed, ("grp", "tok"), 0, 0, tiled=True)
    summed = pl.pallas_call(
        partial(chain_kernel, backward),
        out_shape=shape_of(landed.shape, f32),
        compiler_params=pltpu.CompilerParams(vmem_limit_bytes=grant),
    )(landed)
    home = lax.all_to_all(summed, ("grp", "tok"), 0, 0, tiled=True)
    return home[:, :share].reshape(state.shape), home[:, share, :spare].reshape(norm.shape)


def reduce_vectors(stack):
    grp_size, tok_size = sizes()
    count, length = stack.shape
    share = length // tok_size
    blocks = stack.reshape(count, tok_size, share).transpose(1, 0, 2)
    blocks = blocks.reshape(tok_size, count * share)
    spread = jnp.broadcast_to(blocks[None], (grp_size,) + blocks.shape)
    spread = spread.reshape(grp_size * tok_size, count * share)
    landed = lax.all_to_all(spread, ("grp", "tok"), 0, 0, tiled=True)
    return jnp.sum(landed, axis=0).reshape(count, share)


def on_device(
    layer_input,
    doc_starts,
    ln1_gain,
    ln1_shift,
    w_qkv,
    feat_q,
    feat_k,
    w_out,
    ln2_gain,
    ln2_shift,
    w_fc,
    w_proj,
    cotangent,
):
    tokens, width = layer_input.shape
    head_dim = feat_q.shape[1]
    heads = width // head_dim
    feats = 2 * head_dim
    hidden = w_fc.shape[1]
    rows = min(256, tokens)
    blocks = tokens // rows
    gain1, shift1 = (ln1_gain[None], ln1_shift[None])
    gain2, shift2 = (ln2_gain[None], ln2_shift[None])

    at = jnp.arange(tokens, dtype=jnp.int32)
    marked = (doc_starts[:, None] > 0) & (at[:, None] <= at[None, :])
    last = jnp.max(jnp.where(marked, at[:, None], -1), axis=0)
    start = jnp.maximum(last, 0)[None]
    opened = (last < 0).astype(f32)[None]
    tail = (at >= last[-1]).astype(f32)[None]
    keep = (last[-1] < 0).astype(f32)

    hid1, qkv, phi_q, phi_k, state, norm = call(
        enter_kernel, blocks,
        [down(rows, width), whole((1, width)), whole((1, width)), whole(w_qkv.shape),
         whole(feat_q.shape), whole(feat_k.shape), across(1, rows)],
        [down(rows, width), across(3 * width, rows), across(2 * width, rows), across(2 * width, rows),
         whole((width, feats)), whole((heads, feats))],
        [shape_of((tokens, width), bf16), shape_of((3 * width, tokens), bf16),
         shape_of((2 * width, tokens), bf16), shape_of((2 * width, tokens), bf16),
         shape_of((width, feats), f32), shape_of((heads, feats), f32)],
        (layer_input, gain1, shift1, w_qkv, feat_q, feat_k, tail.astype(bf16)),
    )
    state_in, norm_in = carry_scan(state, norm, keep, False)
    part = heads // 2
    locals_ = [
        call(
            local_kernel, part,
            [head_rows(feats, tokens, at * part), head_rows(feats, tokens, at * part),
             head_rows(head_dim, tokens, 2 * heads + at * part), whole((1, tokens))],
            [head_rows(head_dim, tokens), one_head(tokens)],
            [shape_of((width // 2, tokens), f32), shape_of((part, 1, tokens), f32)],
            (phi_q, phi_k, qkv, start),
        )
        for at in range(2)
    ]
    mixed, mixed_low, denom, resid, hid2, act, slope = call(
        mix_kernel, blocks,
        [across(width // 2, rows), across(width // 2, rows), heads_across(part, rows),
         heads_across(part, rows), across(2 * width, rows), whole((width, feats)),
         whole((heads, feats)), across(1, rows), down(rows, width), whole(w_out.shape),
         whole((1, width)), whole((1, width)), whole(w_fc.shape)],
        [across(width, rows), across(width, rows), heads_across(heads, rows), down(rows, width),
         down(rows, width), down(rows, hidden), down(rows, hidden)],
        [shape_of((width, tokens), f32), shape_of((width, tokens), bf16),
         shape_of((heads, 1, tokens), f32), shape_of((tokens, width), f32),
         shape_of((tokens, width), bf16), shape_of((tokens, hidden), bf16),
         shape_of((tokens, hidden), bf16)],
        (locals_[0][0], locals_[1][0], locals_[0][1], locals_[1][1], phi_q, state_in, norm_in, opened, layer_input, w_out, gain2, shift2, w_fc),
    )
    half = width // 2
    pair = lambda rows, columns: pl.BlockSpec((rows, columns), lambda i, t: (0, i))
    mine_a, theirs_a = tables_of((0, 1))
    mine_b, theirs_b = tables_of((2, 0))
    mine_c, theirs_c = tables_of((1, 2))
    mine_d, theirs_d = tables_of((0, 1))
    last_at = mine_a.shape[0] - 1
    right_half = lambda columns: pl.BlockSpec((tokens, columns), lambda i, t: (0, t[last_at]))
    plain = lambda rows_: pl.BlockSpec((rows_, tokens), lambda i, t: (0, 0))
    chosen = lambda which: pl.BlockSpec((1, half, tokens), lambda i, t: (which, t[last_at], 0))

    def group_a(table, other=None):
        return products(
            table, ((0, 0),), (act, cotangent), (pair(tokens, half), right_half(half)),
            hidden, half, half, None, other,
        )

    other_a = swap_cores(group_a(theirs_a))
    (dpre,) = call(
        slope_kernel, blocks,
        [down(rows, hidden), down(rows, width), whole(w_proj.shape)],
        [down(rows, hidden)],
        [shape_of((tokens, hidden), bf16)],
        (slope, cotangent, w_proj),
    )
    keep_a, give_a = group_a(mine_a, other_a)

    def group_b(table, other=None):
        return products(
            table, ((0, 0),), (hid2, dpre), (pair(tokens, half), right_half(hidden // 2)),
            width, half, hidden // 2, None, other,
        )

    other_b = swap_cores(group_b(theirs_b))
    (output,) = call(
        out_kernel, blocks,
        [down(rows, hidden), down(rows, width), whole(w_proj.shape)],
        [down(rows, width)],
        [shape_of((tokens, width), bf16)],
        (act, resid, w_proj),
    )
    keep_b, give_b = group_b(mine_b, other_b)
    dbranch, dresid, dnum, dden, back_state, back_norm, sums2 = call(
        back_kernel, blocks,
        [down(rows, hidden), down(rows, width), down(rows, width), whole(w_fc.shape), whole((1, width)),
         whole(w_out.shape), across(width, rows), heads_across(heads, rows), across(2 * width, rows),
         across(1, rows)],
        [down(rows, width), down(rows, width), across(width, rows), heads_across(heads, rows),
         whole((width, feats)), whole((heads, feats)), whole((8, width))],
        [shape_of((tokens, width), bf16), shape_of((tokens, width), f32),
         shape_of((width, tokens), f32), shape_of((heads, 1, tokens), f32),
         shape_of((width, feats), f32), shape_of((heads, feats), f32), shape_of((8, width), f32)],
        (dpre, resid, cotangent, w_fc, gain2, w_out, mixed, denom, phi_q, opened),
    )
    state_back, norm_back_in = carry_scan(back_state, back_norm, keep, True)
    split = [
        call(
            local_back_kernel, part,
            [head_rows(feats, tokens, at * part), head_rows(feats, tokens, at * part),
             head_rows(head_dim, tokens, at * part), head_rows(head_dim, tokens, 2 * heads + at * part),
             head_rows(head_dim, tokens, at * part), one_head(tokens, at * part),
             whole((1, tokens)), whole((1, tokens)), head_rows(head_dim, feats, at * part),
             one_head(feats, at * part), head_rows(head_dim, head_dim, at * part)],
            [head_rows(head_dim, tokens), pl.BlockSpec((1, head_dim, head_dim), lambda i: (i, 0, 0)),
             head_rows(feats, tokens), head_rows(head_dim, tokens)],
            [shape_of((width // 2, tokens), bf16), shape_of((part, head_dim, head_dim), f32),
             shape_of((width, tokens), f32), shape_of((width // 2, tokens), f32)],
            (phi_q, phi_k, qkv, qkv, dnum, dden, start, opened, state_in, norm_in[:, None], feat_q),
        )
        for at in range(2)
    ]
    gfq = jnp.concatenate([split[0][1], split[1][1]], axis=0)
    lower = lambda rows_: pl.BlockSpec((rows_, tokens), lambda i: (jnp.minimum(i, part - 1), 0))
    upper = lambda rows_: pl.BlockSpec((rows_, tokens), lambda i: (jnp.maximum(i - part, 0), 0))
    dkv, gfk = call(
        key_back_kernel, heads,
        [head_rows(feats, tokens), head_rows(head_dim, tokens, heads),
         head_rows(head_dim, tokens, 2 * heads), lower(feats), upper(feats), lower(head_dim), upper(head_dim),
         whole((1, tokens)), head_rows(head_dim, feats), one_head(feats), head_rows(head_dim, head_dim)],
        [pl.BlockSpec((2, head_dim, tokens), lambda i: (0, i, 0)),
         pl.BlockSpec((1, head_dim, head_dim), lambda i: (i, 0, 0))],
        [shape_of((2, width, tokens), bf16), shape_of((heads, head_dim, head_dim), f32)],
        (phi_k, qkv, qkv, split[0][2], split[1][2], split[0][3], split[1][3], tail, state_back, norm_back_in[:, None], feat_k),
    )
    grad_input, sums1 = call(
        leave_kernel, blocks,
        [across(width // 2, rows), across(width // 2, rows),
         pl.BlockSpec((2, width, rows), lambda i: (0, 0, i)), whole(w_qkv.shape),
         down(rows, width), whole((1, width)), down(rows, width)],
        [down(rows, width), whole((8, width))],
        [shape_of((tokens, width), f32), shape_of((8, width), f32)],
        (split[0][0], split[1][0], dkv, w_qkv, layer_input, gain1, dresid),
    )

    first_core = lax.axis_index("grp") % 2 == 0

    def group_c(table, flip, other=None):
        chosen_q = jnp.where(first_core != flip, split[0][0], split[1][0])
        return products(
            table, ((1, 0), (0, 1)), (mixed_low, dbranch, hid1, chosen_q),
            (pl.BlockSpec((half, tokens), lambda i, t: (i, 0)), right_half(half), pair(tokens, half),
             plain(half)),
            width, half, 2 * half, None, other,
        )

    other_c = swap_cores(group_c(theirs_c, True))
    keep_c, give_c = group_c(mine_c, False, other_c)
    feats_both = jnp.stack([gfq.reshape(width, head_dim), gfk.reshape(width, head_dim)])
    feats_both = jnp.pad(feats_both, ((0, 0), (0, 0), (0, feats - head_dim)))

    def group_d(table, other=None):
        return products(
            table, ((0, 1), (0, 1)), (hid1, dkv, hid1, dkv),
            (pair(tokens, half), chosen(0), pair(tokens, half), chosen(1)),
            width, half, 2 * half + feats, feats_both, other,
        )

    other_d = swap_cores(group_d(theirs_d))
    keep_d, give_d = group_d(mine_d, other_d)
    vectors = reduce_vectors(jnp.concatenate([sums1[:2], sums2[:2]], axis=0))
    grad_proj = jnp.concatenate(fold(keep_a, give_a, (0, 1)), axis=1)
    grad_fc = jnp.concatenate(fold(keep_b, give_b, (2, 0)), axis=1)
    c_pair = fold(keep_c, give_c, (1, 2))
    d_pair = fold(keep_d, give_d, (0, 1))
    grad_out = jnp.concatenate([part[:, :half] for part in c_pair], axis=1)
    grad_qkv = jnp.concatenate(
        [part[:, half:] for part in c_pair]
        + [part[:, :half] for part in d_pair]
        + [part[:, half : 2 * half] for part in d_pair],
        axis=1,
    )
    return (
        output,
        grad_input,
        vectors[0],
        vectors[1],
        grad_qkv,
        d_pair[0][:, 2 * half : 2 * half + head_dim],
        d_pair[1][:, 2 * half : 2 * half + head_dim],
        grad_out,
        vectors[2],
        vectors[3],
        grad_fc,
        grad_proj,
    )


def solution(mesh):
    in_specs = (
        P(("grp", "tok"), None),
        P(("grp", "tok")),
        P(),
        P(),
        P(),
        P(),
        P(),
        P(),
        P(),
        P(),
        P(),
        P(),
        P(("grp", "tok"), None),
    )
    out_specs = (
        P(("grp", "tok"), None),
        P(("grp", "tok"), None),
        P("tok"),
        P("tok"),
        P("tok", None),
        P("tok", None),
        P("tok", None),
        P("tok", None),
        P("tok"),
        P("tok"),
        P("tok", None),
        P("tok", None),
    )

    return jax.shard_map(on_device, mesh=mesh, in_specs=in_specs, out_specs=out_specs, check_vma=False)
```

profile of v0, /device:TPU:0, one launch (start us, length us, event | category | flops | bytes accessed | tf_op | source)
XLA Modules:
  0.0 494.4 jit_solution(8581060413781090355)
XLA Ops:
  9.5 24.4 %shard_map.292 = (bf16[1024,768]{1,0:T(8,128)(2,1)}, bf16[2304,1024]{1,0:T(8,128)(2,1)}, bf16[1536,1024]{1,0:T(8,128)(2,1)}, bf16[1536,1024]{1,0:T(8,128)(2,1)}, f32[768,128]{1,0:T(8,128)}, /*index=5*/f32[12,128]{1,0:T(8,128)}) custom-call(bf16[1024,768]{1,0:T(8,128)(2,1)} %x_ref.5, f32[1,768]{1,0:T(1,128)} %broadcast_in_dim.32.gain_ref, ...), custom_call_target="tpu_custom_call" | custom-call | tf_op jit(solution)/shard_map/pallas_call | solution.py:313
  36.6 23.5 %all_to_all.29.got_ref = f32[32,25,128]{2,1,0:T(8,128)} all-to-all(f32[32,25,128]{2,1,0:T(8,128)S(1)} %pad_maximum_fusion.4), channel_id=1, replica_groups=mesh['grp'=4,'tok'=8] {'grp','tok'}, dimensions={0} | all-to-all | bytes 819200 | tf_op jit(solution)/shard_map/all_to_all | solution.py:507
  60.0 5.1 %shard_map.295 = f32[32,25,128]{2,1,0:T(8,128)} custom-call(f32[32,25,128]{2,1,0:T(8,128)} %all_to_all.29.got_ref), custom_call_target="tpu_custom_call" | custom-call | tf_op jit(solution)/shard_map/pallas_call | solution.py:508
  68.5 10.2 %shard_map.294 = (f32[384,1024]{1,0:T(8,128)}, f32[6,1,1024]{2,1,0:T(1,128)}) custom-call(bf16[1536,1024]{1,0:T(8,128)(2,1)} %get-tuple-element.56.pq_ref, bf16[1536,1024]{1,0:T(8,128)(2,1)} %get-tuple-element.57.pk_ref, bf16[2304,1024]{1,0:T(8,128)(2,1)} %get-tuple-element.58.v_ref.q_ref.k_ref, s32[1,1024]{1,0:T(1,128)} %bitcast.50), custom_call_target="tpu_custom_call" | custom-call | tf_op jit(solution)/shard_map/pallas_call | solution.py:313
  78.7 10.2 %shard_map.293 = (f32[384,1024]{1,0:T(8,128)}, f32[6,1,1024]{2,1,0:T(1,128)}) custom-call(bf16[1536,1024]{1,0:T(8,128)(2,1)} %get-tuple-element.56.pq_ref, bf16[1536,1024]{1,0:T(8,128)(2,1)} %get-tuple-element.57.pk_ref, bf16[2304,1024]{1,0:T(8,128)(2,1)} %get-tuple-element.58.v_ref.q_ref.k_ref, s32[1,1024]{1,0:T(1,128)} %bitcast.51), custom_call_target="tpu_custom_call" | custom-call | tf_op jit(solution)/shard_map/pallas_call | solution.py:313
  92.2 22.0 %shard_map.296 = (f32[768,1024]{1,0:T(8,128)}, bf16[768,1024]{1,0:T(8,128)(2,1)}, f32[12,1,1024]{2,1,0:T(1,128)}, f32[1024,768]{1,0:T(8,128)}, bf16[1024,768]{1,...) custom-call(f32[384,1024]{1,0:T(8,128)} %get-tuple-element.59.num0_ref, ...), custom_call_target="tpu_custom_call" | custom-call | tf_op jit(solution)/shard_map/pallas_call | solution.py:313
  114.3 11.1 %shard_map.298.dpre_ref.refs_1_ = bf16[1024,3072]{1,0:T(8,128)(2,1)} custom-call(bf16[1024,3072]{1,0:T(8,128)(2,1)} %get-tuple-element.67.slope_ref, bf16[1024,768]{1,0:T(8,128)(2,1)} %refs_1_.3, bf16[3072,768]{1,0:T(8,128)(2,1)} %wproj_ref.3), custom_call_target="tpu_custom_call" | custom-call | tf_op jit(solution)/shard_map/pallas_call | solution.py:313
  125.4 18.3 %shard_map.299 = (bf16[1024,768]{1,0:T(8,128)(2,1)}, f32[1024,768]{1,0:T(8,128)}, f32[768,1024]{1,0:T(8,128)}, f32[12,1,1024]{2,1,0:T(1,128)}, f32[768,128]{1,0:...) custom-call(bf16[1024,3072]{1,0:T(8,128)(2,1)} %shard_map.298.dpre_ref.refs_1_, f32[1024,768]{1,0:T(8,128)} %get-tuple-element.66.resid_ref, ...), custom_call_target="tpu_custom_call" | custom-call | tf_op jit(solution)/shard_map/pallas_call | solution.py:313
  146.3 5.9 %all-to-all-start.2 = ((f32[32,25,128]{2,1,0:T(8,128)}), f32[32,25,128]{2,1,0:T(8,128)S(1)}, u32[]{:S(2)}, u32[]{:S(2)}) async-start(f32[32,25,128]{2,1,0:T(8,128)} %pad_maximum_fusion.5), calls=%async_computation.2 | async-start | bytes 1048576 | tf_op jit(solution)/shard_map/all_to_all | solution.py:507
  161.1 18.8 %shard_map.301 = (bf16[384,1024]{1,0:T(8,128)(2,1)}, f32[6,64,64]{2,1,0:T(8,128)}, f32[768,1024]{1,0:T(8,128)}, f32[384,1024]{1,0:T(8,128)}) custom-call(bf16[1536,1024]{1,0:T(8,128)(2,1)} %get-tuple-element.56.pq_ref, bf16[1536,1024]{1,0:T(8,128)(2,1)} %get-tuple-element.57.pk_ref, bf16[2304,1024]{1,0:T(8,128)(2,1)} %get-tuple-element.58.v_ref.q_ref.k_ref, ...), custom_call_target="tpu_custom_call" | custom-call | tf_op jit(solution)/shard_map/pallas_call | solution.py:313
  179.9 18.8 %shard_map.300 = (bf16[384,1024]{1,0:T(8,128)(2,1)}, f32[6,64,64]{2,1,0:T(8,128)}, f32[768,1024]{1,0:T(8,128)}, f32[384,1024]{1,0:T(8,128)}) custom-call(bf16[1536,1024]{1,0:T(8,128)(2,1)} %get-tuple-element.56.pq_ref, bf16[1536,1024]{1,0:T(8,128)(2,1)} %get-tuple-element.57.pk_ref, bf16[2304,1024]{1,0:T(8,128)(2,1)} %get-tuple-element.58.v_ref.q_ref.k_ref, ...), custom_call_target="tpu_custom_call" | custom-call | tf_op jit(solution)/shard_map/pallas_call | solution.py:313
  199.5 5.1 %shard_map.302 = f32[32,25,128]{2,1,0:T(8,128)} custom-call(f32[32,25,128]{2,1,0:T(8,128)} %copy-done.6), custom_call_target="tpu_custom_call" | custom-call | tf_op jit(solution)/shard_map/pallas_call | solution.py:508
  204.6 5.6 %all-to-all-start.3 = ((f32[32,25,128]{2,1,0:T(8,128)}), f32[32,25,128]{2,1,0:T(8,128)S(1)}, u32[]{:S(2)}, u32[]{:S(2)}) async-start(f32[32,25,128]{2,1,0:T(8,128)} %shard_map.302), calls=%async_computation.3 | async-start | bytes 1048576 | tf_op jit(solution)/shard_map/all_to_all | solution.py:513
  211.6 6.0 %shard_map.305 = f32[16,48,768]{2,1,0:T(8,128)} custom-call(s32[17]{0:T(128)} %pad_add_fusion.1.table_ref, bf16[768,1024]{1,0:T(8,128)(2,1)} %get-tuple-element.85.refs_0_, bf16[1024,768]{1,0:T(8,128)(2,1)} %get-tuple-element.86.refs_1_, bf16[1024,768]{1,0:T(8,128)(2,1)} %get-tuple-element.87.refs_2_.refs_0_, bf16[384,1024]{1,0:T(8,128)(2,1)} %get-tuple-element.160.refs_3_), custom_call_target="tpu_custom_call" | custom-call | tf_op jit(solution)/shard_map/pallas_call | solution.py:441
  219.6 10.9 %shard_map.311 = f32[16,192,384]{2,1,0:T(8,128)} custom-call(s32[17]{0:T(128)} %pad_add_fusion.3.table_ref, bf16[1024,3072]{1,0:T(8,128)(2,1)} %get-tuple-element.65.act_ref.refs_0_, bf16[1024,768]{1,0:T(8,128)(2,1)} %refs_1_.3), custom_call_target="tpu_custom_call" | custom-call | tf_op jit(solution)/shard_map/pallas_call | solution.py:441
  232.3 14.0 %shard_map.303 = (bf16[2,768,1024]{2,1,0:T(8,128)(2,1)}, f32[12,64,64]{2,1,0:T(8,128)}) custom-call(bf16[1536,1024]{1,0:T(8,128)(2,1)} %get-tuple-element.57.pk_ref, bf16[2304,1024]{1,0:T(8,128)(2,1)} %get-tuple-element.58.v_ref.q_ref.k_ref, bf16[2304,1024]{1,0:T(8,128)(2,1)} %get-tuple-element.58.v_ref.q_ref.k_ref, ...), custom_call_target="tpu_custom_call" | custom-call | tf_op jit(solution)/shard_map/pallas_call | solution.py:313
  248.3 6.4 %shard_map.307 = f32[16,48,896]{2,1,0:T(8,128)} custom-call(s32[17]{0:T(128)} %pad_add_fusion.3.table_ref, bf16[1024,768]{1,0:T(8,128)(2,1)} %get-tuple-element.87.refs_2_.refs_0_, bf16[2,768,1024]{2,1,0:T(8,128)(2,1)} %get-tuple-element.80.dkv_ref.refs_1_.refs_3_, bf16[1024,768]{1,0:T(8,128)(2,1)} %get-tuple-element.87.refs_2_.refs_0_, ...), custom_call_target="tpu_custom_call" | custom-call | tf_op jit(solution)/shard_map/pallas_call | solution.py:441
  255.6 7.9 %shard_map.309 = f32[16,48,1536]{2,1,0:T(8,128)} custom-call(s32[17]{0:T(128)} %pad_add_fusion.5.table_ref, bf16[1024,768]{1,0:T(8,128)(2,1)} %get-tuple-element.95.refs_0_, bf16[1024,3072]{1,0:T(8,128)(2,1)} %shard_map.298.dpre_ref.refs_1_), custom_call_target="tpu_custom_call" | custom-call | tf_op jit(solution)/shard_map/pallas_call | solution.py:441
  264.3 7.2 %shard_map.306 = (f32[8,48,768]{2,1,0:T(8,128)}, f32[8,48,768]{2,1,0:T(8,128)}) custom-call(s32[17]{0:T(128)} %get-tuple-element.212.table_ref, bf16[768,1024]{1,0:T(8,128)(2,1)} %get-tuple-element.85.refs_0_, bf16[1024,768]{1,0:T(8,128)(2,1)} %get-tuple-element.86.refs_1_, bf16[1024,768]{1,0:T(8,128)(2,1)} %get-tuple-element.87.refs_2_.refs_0_, ...), custom_call_target="tpu_custom_call" | custom-call | tf_op jit(solution)/shard_map/pallas_call | solution.py:441
  274.8 8.0 %shard_map.308 = (f32[8,48,896]{2,1,0:T(8,128)}, f32[8,48,896]{2,1,0:T(8,128)}) custom-call(s32[17]{0:T(128)} %get-tuple-element.213.table_ref, bf16[1024,768]{1,0:T(8,128)(2,1)} %get-tuple-element.87.refs_2_.refs_0_, bf16[2,768,1024]{2,1,0:T(8,128)(2,1)} %get-tuple-element.80.dkv_ref.refs_1_.refs_3_, bf16[1024,768]{1,0:T(8,128)(2,1)} %get-tuple-element.87.refs_2_.refs_0_, ...), custom_call_target="tpu_custom_call" | custom-call | tf_op jit(solution)/shard_map/pallas_call | solution.py:441
  284.3 6.1 %collective-permute-done.1 = f32[8,48,768]{2,1,0:T(8,128)} collective-permute-done((f32[8,48,768]{2,1,0:T(8,128)}, f32[8,48,768]{2,1,0:T(8,128)}, u32[]{:S(2)}, u32[]{:S(2)}) %collective-permute-start.1) | collective-permute-done | bytes 1179680 | tf_op jit(solution)/shard_map/ppermute | solution.py:454
  295.4 7.9 %collective-permute-done.2 = f32[4,48,768]{2,1,0:T(8,128)S(1)} collective-permute-done((f32[4,48,768]{2,1,0:T(8,128)S(1)}, f32[4,48,768]{2,1,0:T(8,128)S(1)}, u32[]{:S(2)}, u32[]{:S(2)}) %collective-permute-start.2) | collective-permute-done | bytes 589856 | tf_op jit(solution)/shard_map/ppermute | solution.py:454
  306.1 10.1 %shard_map.304 = (f32[1024,768]{1,0:T(8,128)}, f32[8,768]{1,0:T(8,128)}) custom-call(bf16[384,1024]{1,0:T(8,128)(2,1)} %get-tuple-element.72.dq0_ref, bf16[384,1024]{1,0:T(8,128)(2,1)} %get-tuple-element.73.dq1_ref, bf16[2,768,1024]{2,1,0:T(8,128)(2,1)} %get-tuple-element.80.dkv_ref.refs_1_.refs_3_, bf16[768,2304]{1,0:T(8,128)(2,1)} %w_ref.3, ...), custom_call_target="tpu_custom_call" | custom-call | tf_op jit(solution)/shard_map/pallas_call | solution.py:313
  319.5 12.7 %shard_map.312 = (f32[8,192,384]{2,1,0:T(8,128)}, f32[8,192,384]{2,1,0:T(8,128)}) custom-call(s32[17]{0:T(128)} %get-tuple-element.213.table_ref, bf16[1024,3072]{1,0:T(8,128)(2,1)} %get-tuple-element.65.act_ref.refs_0_, bf16[1024,768]{1,0:T(8,128)(2,1)} %refs_1_.3, f32[16,192,384]{2,1,0:T(8,128)} %collective-permute-done.21.refs_2_), custom_call_target="tpu_custom_call" | custom-call | tf_op jit(solution)/shard_map/pallas_call | solution.py:441
  341.6 9.9 %shard_map.310 = (f32[8,48,1536]{2,1,0:T(8,128)}, f32[8,48,1536]{2,1,0:T(8,128)}) custom-call(s32[17]{0:T(128)} %pad_add_fusion.4.table_ref, bf16[1024,768]{1,0:T(8,128)(2,1)} %get-tuple-element.95.refs_0_, bf16[1024,3072]{1,0:T(8,128)(2,1)} %shard_map.298.dpre_ref.refs_1_, f32[16,48,1536]{2,1,0:T(8,128)} %copy-done), custom_call_target="tpu_custom_call" | custom-call | tf_op jit(solution)/shard_map/pallas_call | solution.py:441
  357.2 10.4 %shard_map.297 = bf16[1024,768]{1,0:T(8,128)(2,1)} custom-call(bf16[1024,3072]{1,0:T(8,128)(2,1)} %get-tuple-element.65.act_ref.refs_0_, f32[1024,768]{1,0:T(8,128)} %get-tuple-element.66.resid_ref, bf16[3072,768]{1,0:T(8,128)(2,1)} %wproj_ref.3), custom_call_target="tpu_custom_call" | custom-call | tf_op jit(solution)/shard_map/pallas_call | solution.py:313
  367.6 23.5 %all-to-all-done.4 = f32[32,1,384]{2,1,0:T(1,128)S(1)} async-done(((f32[32,1,384]{2,1,0:T(1,128)}), f32[32,1,384]{2,1,0:T(1,128)S(1)}, u32[]{:S(2)}, u32[]{:S(2)}) %all-to-all-start.4) | async-done | bytes 49184 | tf_op jit(solution)/shard_map/all_to_all | solution.py:525
  396.2 4.6 collective-permute-done.10
  401.3 10.0 %collective-permute-done.11 = f32[1,48,896]{2,1,0:T(8,128)S(1)} collective-permute-done((f32[1,48,896]{2,1,0:T(8,128)S(1)}, f32[1,48,896]{2,1,0:T(8,128)S(1)}, u32[]{:S(2)}, u32[]{:S(2)}) %collective-permute-start.11) | collective-permute-done | bytes 172064 | tf_op jit(solution)/shard_map/ppermute | solution.py:454
  419.0 21.5 %collective-permute-done.23 = f32[4,192,384]{2,1,0:T(8,128)S(1)} collective-permute-done((f32[4,192,384]{2,1,0:T(8,128)S(1)}, f32[4,192,384]{2,1,0:T(8,128)S(1)}, u32[]{:S(2)}, u32[]{:S(2)}) %collective-permute-start.23) | collective-permute-done | bytes 1179680 | tf_op jit(solution)/shard_map/ppermute | solution.py:454
  441.5 18.1 %collective-permute-done.24 = f32[2,192,384]{2,1,0:T(8,128)S(1)} collective-permute-done((f32[2,192,384]{2,1,0:T(8,128)S(1)}, f32[2,192,384]{2,1,0:T(8,128)S(1)}, u32[]{:S(2)}, u32[]{:S(2)}) %collective-permute-start.24) | collective-permute-done | bytes 589856 | tf_op jit(solution)/shard_map/ppermute | solution.py:454
  465.1 12.8 %collective-permute-done.25 = f32[1,192,384]{2,1,0:T(8,128)} collective-permute-done((f32[1,192,384]{2,1,0:T(8,128)S(1)}, f32[1,192,384]{2,1,0:T(8,128)}, u32[]{:S(2)}, u32[]{:S(2)}) %collective-permute-start.25) | collective-permute-done | bytes 294944 | tf_op jit(solution)/shard_map/ppermute | solution.py:454
  (184 shorter events, 105.8 us)
Async XLA Ops:
  65.1 25.6 %all-to-all-start.1 = ((f32[32,25,128]{2,1,0:T(8,128)}), f32[32,25,128]{2,1,0:T(8,128)S(1)}, u32[]{:S(2)}, u32[]{:S(2)}) async-start(f32[32,25,128]{2,1,0:T(8,128)} %shard_map.295), calls=%async_computation.1 | async-start | bytes 1048576 | tf_op jit(solution)/shard_map/all_to_all | solution.py:513
  146.3 52.4 %all-to-all-start.2 = ((f32[32,25,128]{2,1,0:T(8,128)}), f32[32,25,128]{2,1,0:T(8,128)S(1)}, u32[]{:S(2)}, u32[]{:S(2)}) async-start(f32[32,25,128]{2,1,0:T(8,128)} %pad_maximum_fusion.5), calls=%async_computation.2 | async-start | bytes 1048576 | tf_op jit(solution)/shard_map/all_to_all | solution.py:507
  204.6 26.2 %all-to-all-start.3 = ((f32[32,25,128]{2,1,0:T(8,128)}), f32[32,25,128]{2,1,0:T(8,128)S(1)}, u32[]{:S(2)}, u32[]{:S(2)}) async-start(f32[32,25,128]{2,1,0:T(8,128)} %shard_map.302), calls=%async_computation.3 | async-start | bytes 1048576 | tf_op jit(solution)/shard_map/all_to_all | solution.py:513
  217.5 46.8 %collective-permute-start = (f32[16,48,768]{2,1,0:T(8,128)}, f32[16,48,768]{2,1,0:T(8,128)}, u32[]{:S(2)}, u32[]{:S(2)}) collective-permute-start(f32[16,48,768]{2,1,0:T(8,128)} %shard_map.305), channel_id=1, source_target_pairs={{0,8},{1,9},{2,10},{3,11},{4,12},{5,13},{6,14},{7,15},{8,0},{9,1},... | collective-permute-start | bytes 7077896 | tf_op jit(solution)/shard_map/ppermute | solution.py:454
  230.5 89.0 %collective-permute-start.21 = (f32[16,192,384]{2,1,0:T(8,128)}, f32[16,192,384]{2,1,0:T(8,128)}, u32[]{:S(2)}, u32[]{:S(2)}) collective-permute-start(f32[16,192,384]{2,1,0:T(8,128)} %shard_map.311), channel_id=1, source_target_pairs={{0,8},{1,9},{2,10},{3,11},{4,12},{5,13},{6,14},{7,15},{8,0},{9,1},... | collective-permute-start | bytes 14155784 | tf_op jit(solution)/shard_map/ppermute | solution.py:454
  254.7 18.6 %collective-permute-start.7 = (f32[16,48,896]{2,1,0:T(8,128)}, f32[16,48,896]{2,1,0:T(8,128)S(1)}, u32[]{:S(2)}, u32[]{:S(2)}) collective-permute-start(f32[16,48,896]{2,1,0:T(8,128)} %shard_map.307), channel_id=1, source_target_pairs={{0,8},{1,9},{2,10},{3,11},{4,12},{5,13},{6,14},{7,15},{8,0},{9,1},... | collective-permute-start | bytes 8257544 | tf_op jit(solution)/shard_map/ppermute | solution.py:454
  263.6 75.9 %collective-permute-start.14 = (f32[16,48,1536]{2,1,0:T(8,128)}, f32[16,48,1536]{2,1,0:T(8,128)S(1)}, u32[]{:S(2)}, u32[]{:S(2)}) collective-permute-start(f32[16,48,1536]{2,1,0:T(8,128)} %shard_map.309), channel_id=1, source_target_pairs={{0,8},{1,9},{2,10},{3,11},{4,12},{5,13},{6,14},{7,15},{8,0},{9,1},... | collective-permute-start | bytes 14155784 | tf_op jit(solution)/shard_map/ppermute | solution.py:454
  271.5 18.9 %collective-permute-start.1 = (f32[8,48,768]{2,1,0:T(8,128)}, f32[8,48,768]{2,1,0:T(8,128)}, u32[]{:S(2)}, u32[]{:S(2)}) collective-permute-start(f32[8,48,768]{2,1,0:T(8,128)} %get-tuple-element.89), channel_id=1, source_target_pairs={{0,1},{1,0},{2,3},{3,2},{4,5},{5,4},{6,7},{7,6},{8,10},{9,11},{10,... | collective-permute-start | bytes 3538952 | tf_op jit(solution)/shard_map/ppermute | solution.py:454
  282.8 49.9 %collective-permute-start.8 = (f32[8,48,896]{2,1,0:T(8,128)}, f32[8,48,896]{2,1,0:T(8,128)}, u32[]{:S(2)}, u32[]{:S(2)}) collective-permute-start(f32[8,48,896]{2,1,0:T(8,128)} %get-tuple-element.94), channel_id=1, source_target_pairs={{0,16},{1,17},{2,18},{3,19},{4,20},{5,21},{6,22},{7,23},{8,9},{9,8... | collective-permute-start | bytes 4128776 | tf_op jit(solution)/shard_map/ppermute | solution.py:454
  292.2 11.1 %collective-permute-start.2 = (f32[4,48,768]{2,1,0:T(8,128)S(1)}, f32[4,48,768]{2,1,0:T(8,128)S(1)}, u32[]{:S(2)}, u32[]{:S(2)}) collective-permute-start(f32[4,48,768]{2,1,0:T(8,128)S(1)} %get-tuple-element.159), channel_id=1, source_target_pairs={{0,2},{1,3},{2,0},{3,1},{4,6},{5,7},{6,4},{7,5},{8,24},{9,25},{10,... | collective-permute-start | bytes 1769480 | tf_op jit(solution)/shard_map/ppermute | solution.py:454
  303.4 13.5 %collective-permute-start.3 = (f32[2,48,768]{2,1,0:T(8,128)S(1)}, f32[2,48,768]{2,1,0:T(8,128)S(1)}, u32[]{:S(2)}, u32[]{:S(2)}) collective-permute-start(f32[2,48,768]{2,1,0:T(8,128)S(1)} %get-tuple-element.169), channel_id=1, source_target_pairs={{0,16},{1,17},{2,18},{3,19},{4,20},{5,21},{6,22},{7,23},{8,9},{9,8... | collective-permute-start | bytes 884744 | tf_op jit(solution)/shard_map/ppermute | solution.py:454
  316.9 20.0 %collective-permute-start.4 = (f32[1,48,768]{2,1,0:T(8,128)S(1)}, f32[1,48,768]{2,1,0:T(8,128)}, u32[]{:S(2)}, u32[]{:S(2)}) collective-permute-start(f32[1,48,768]{2,1,0:T(8,128)S(1)} %slice_add_fusion.22), channel_id=1, source_target_pairs={{0,4},{1,5},{2,6},{3,7},{4,0},{5,1},{6,2},{7,3},{8,12},{9,13},{10,... | collective-permute-start | bytes 442376 | tf_op jit(solution)/shard_map/ppermute | solution.py:454
  332.2 79.7 %collective-permute-start.22 = (f32[8,192,384]{2,1,0:T(8,128)}, f32[8,192,384]{2,1,0:T(8,128)S(1)}, u32[]{:S(2)}, u32[]{:S(2)}) collective-permute-start(f32[8,192,384]{2,1,0:T(8,128)} %get-tuple-element.99), channel_id=1, source_target_pairs={{0,16},{1,17},{2,18},{3,19},{4,20},{5,21},{6,22},{7,23},{8,9},{9,8... | collective-permute-start | bytes 7077896 | tf_op jit(solution)/shard_map/ppermute | solution.py:454
  335.5 56.8 %collective-permute-start.9 = (f32[4,48,896]{2,1,0:T(8,128)}, f32[4,48,896]{2,1,0:T(8,128)}, u32[]{:S(2)}, u32[]{:S(2)}) collective-permute-start(f32[4,48,896]{2,1,0:T(8,128)} %get-tuple-element.153), channel_id=1, source_target_pairs={{0,1},{1,0},{2,3},{3,2},{4,5},{5,4},{6,7},{7,6},{8,10},{9,11},{10,... | collective-permute-start | bytes 2064392 | tf_op jit(solution)/shard_map/ppermute | solution.py:454
  337.9 53.2 %collective-permute-start.5 = (f32[1,48,768]{2,1,0:T(8,128)S(1)}, f32[1,48,768]{2,1,0:T(8,128)}, u32[]{:S(2)}, u32[]{:S(2)}) collective-permute-start(f32[1,48,768]{2,1,0:T(8,128)S(1)} %fusion.4), channel_id=1, source_target_pairs={{0,16},{1,17},{2,18},{3,19},{4,20},{5,21},{6,22},{7,23},{8,24},{9,... | collective-permute-start | bytes 442376 | tf_op jit(solution)/shard_map/ppermute | solution.py:454
  351.5 61.4 %collective-permute-start.15 = (f32[8,48,1536]{2,1,0:T(8,128)}, f32[8,48,1536]{2,1,0:T(8,128)}, u32[]{:S(2)}, u32[]{:S(2)}) collective-permute-start(f32[8,48,1536]{2,1,0:T(8,128)} %get-tuple-element.97), channel_id=1, source_target_pairs={{0,2},{1,3},{2,0},{3,1},{4,6},{5,7},{6,4},{7,5},{8,24},{9,25},{10,... | collective-permute-start | bytes 7077896 | tf_op jit(solution)/shard_map/ppermute | solution.py:454
  354.4 36.7 %all-to-all-start.4 = ((f32[32,1,384]{2,1,0:T(1,128)}), f32[32,1,384]{2,1,0:T(1,128)S(1)}, u32[]{:S(2)}, u32[]{:S(2)}) async-start(f32[32,1,384]{2,1,0:T(1,128)} %all_to_all.22), calls=%async_computation.4 | async-start | bytes 98304 | tf_op jit(solution)/shard_map/all_to_all | solution.py:525
  392.1 4.0 collective-permute-start.6
  393.4 7.3 %collective-permute-start.10 = (f32[2,48,896]{2,1,0:T(8,128)S(1)}, f32[2,48,896]{2,1,0:T(8,128)S(1)}, u32[]{:S(2)}, u32[]{:S(2)}) collective-permute-start(f32[2,48,896]{2,1,0:T(8,128)S(1)} %get-tuple-element.163), channel_id=1, source_target_pairs={{0,2},{1,3},{2,0},{3,1},{4,6},{5,7},{6,4},{7,5},{8,24},{9,25},{10,... | collective-permute-start | bytes 1032200 | tf_op jit(solution)/shard_map/ppermute | solution.py:454
  400.8 10.5 %collective-permute-start.11 = (f32[1,48,896]{2,1,0:T(8,128)S(1)}, f32[1,48,896]{2,1,0:T(8,128)S(1)}, u32[]{:S(2)}, u32[]{:S(2)}) collective-permute-start(f32[1,48,896]{2,1,0:T(8,128)S(1)} %slice_add_fusion.20), channel_id=1, source_target_pairs={{0,4},{1,5},{2,6},{3,7},{4,0},{5,1},{6,2},{7,3},{8,12},{9,13},{10,... | collective-permute-start | bytes 516104 | tf_op jit(solution)/shard_map/ppermute | solution.py:454
  411.3 5.8 %collective-permute-start.12 = (f32[1,48,896]{2,1,0:T(8,128)S(1)}, f32[1,48,896]{2,1,0:T(8,128)S(1)}, u32[]{:S(2)}, u32[]{:S(2)}) collective-permute-start(f32[1,48,896]{2,1,0:T(8,128)S(1)} %fusion.3), channel_id=1, source_target_pairs={{0,16},{1,17},{2,18},{3,19},{4,20},{5,21},{6,22},{7,23},{8,24},{9,... | collective-permute-start | bytes 516104 | tf_op jit(solution)/shard_map/ppermute | solution.py:454
  412.3 28.2 %collective-permute-start.23 = (f32[4,192,384]{2,1,0:T(8,128)S(1)}, f32[4,192,384]{2,1,0:T(8,128)S(1)}, u32[]{:S(2)}, u32[]{:S(2)}) collective-permute-start(f32[4,192,384]{2,1,0:T(8,128)S(1)} %get-tuple-element.149), channel_id=1, source_target_pairs={{0,1},{1,0},{2,3},{3,2},{4,5},{5,4},{6,7},{7,6},{8,10},{9,11},{10,... | collective-permute-start | bytes 3538952 | tf_op jit(solution)/shard_map/ppermute | solution.py:454
  415.6 25.1 %collective-permute-start.16 = (f32[4,48,1536]{2,1,0:T(8,128)S(1)}, f32[4,48,1536]{2,1,0:T(8,128)S(1)}, u32[]{:S(2)}, u32[]{:S(2)}) collective-permute-start(f32[4,48,1536]{2,1,0:T(8,128)S(1)} %get-tuple-element.151), channel_id=1, source_target_pairs={{0,16},{1,17},{2,18},{3,19},{4,20},{5,21},{6,22},{7,23},{8,9},{9,8... | collective-permute-start | bytes 3538952 | tf_op jit(solution)/shard_map/ppermute | solution.py:454
  417.2 1.7 collective-permute-start.13
  440.6 19.1 %collective-permute-start.24 = (f32[2,192,384]{2,1,0:T(8,128)S(1)}, f32[2,192,384]{2,1,0:T(8,128)S(1)}, u32[]{:S(2)}, u32[]{:S(2)}) collective-permute-start(f32[2,192,384]{2,1,0:T(8,128)S(1)} %get-tuple-element.155), channel_id=1, source_target_pairs={{0,2},{1,3},{2,0},{3,1},{4,6},{5,7},{6,4},{7,5},{8,24},{9,25},{10,... | collective-permute-start | bytes 1769480 | tf_op jit(solution)/shard_map/ppermute | solution.py:454
  440.8 18.9 %collective-permute-start.17 = (f32[2,48,1536]{2,1,0:T(8,128)S(1)}, f32[2,48,1536]{2,1,0:T(8,128)S(1)}, u32[]{:S(2)}, u32[]{:S(2)}) collective-permute-start(f32[2,48,1536]{2,1,0:T(8,128)S(1)} %get-tuple-element.157), channel_id=1, source_target_pairs={{0,1},{1,0},{2,3},{3,2},{4,5},{5,4},{6,7},{7,6},{8,10},{9,11},{10,... | collective-permute-start | bytes 1769480 | tf_op jit(solution)/shard_map/ppermute | solution.py:454
  459.6 18.2 %collective-permute-start.25 = (f32[1,192,384]{2,1,0:T(8,128)S(1)}, f32[1,192,384]{2,1,0:T(8,128)}, u32[]{:S(2)}, u32[]{:S(2)}) collective-permute-start(f32[1,192,384]{2,1,0:T(8,128)S(1)} %slice_add_fusion.14), channel_id=1, source_target_pairs={{0,4},{1,5},{2,6},{3,7},{4,0},{5,1},{6,2},{7,3},{8,12},{9,13},{10,... | collective-permute-start | bytes 884744 | tf_op jit(solution)/shard_map/ppermute | solution.py:454
  459.8 21.2 %collective-permute-start.18 = (f32[1,48,1536]{2,1,0:T(8,128)S(1)}, f32[1,48,1536]{2,1,0:T(8,128)}, u32[]{:S(2)}, u32[]{:S(2)}) collective-permute-start(f32[1,48,1536]{2,1,0:T(8,128)S(1)} %slice_add_fusion.16), channel_id=1, source_target_pairs={{0,4},{1,5},{2,6},{3,7},{4,0},{5,1},{6,2},{7,3},{8,12},{9,13},{10,... | collective-permute-start | bytes 884744 | tf_op jit(solution)/shard_map/ppermute | solution.py:454
  478.8 9.0 %collective-permute-start.26 = (f32[1,192,384]{2,1,0:T(8,128)S(1)}, f32[1,192,384]{2,1,0:T(8,128)S(1)}, u32[]{:S(2)}, u32[]{:S(2)}) collective-permute-start(f32[1,192,384]{2,1,0:T(8,128)S(1)} %fusion.1), channel_id=1, source_target_pairs={{0,16},{1,17},{2,18},{3,19},{4,20},{5,21},{6,22},{7,23},{8,24},{9,... | collective-permute-start | bytes 884744 | tf_op jit(solution)/shard_map/ppermute | solution.py:454
  482.0 9.0 %collective-permute-start.19 = (f32[1,48,1536]{2,1,0:T(8,128)S(1)}, f32[1,48,1536]{2,1,0:T(8,128)S(1)}, u32[]{:S(2)}, u32[]{:S(2)}) collective-permute-start(f32[1,48,1536]{2,1,0:T(8,128)S(1)} %fusion.2), channel_id=1, source_target_pairs={{0,16},{1,17},{2,18},{3,19},{4,20},{5,21},{6,22},{7,23},{8,24},{9,... | collective-permute-start | bytes 884744 | tf_op jit(solution)/shard_map/ppermute | solution.py:454
  487.9 3.9 collective-permute-start.27
  491.1 2.1 collective-permute-start.20
  (17 other events, 137.4 us)
where the time goes:
time: 497 us; the launch traced here: 494 us
  Pallas kernels  247 us (50%)
  waiting for transfers between devices  113 us (23%)
  starting transfers between devices  46.8 us (9%)
  other arithmetic  33.7 us (7%)
  local copies, waits for them, and re-layouts  27.8 us (6%)
  blocking collectives  23.5 us (5%)
    pallas_call x11, Pallas kernels, call(): pl.pallas_call(kernel, grid=(grid,), in_specs=ins, out_specs=outs, out_sh...  168 us
    ppermute x28, waiting for transfers between devices, send(): return lax.ppermute(value, ('grp', 'tok'), flips(first, second))  89.8 us
    pallas_call x8, Pallas kernels, products(): pl.pallas_call(partial(product_kernel, forms, tail is not None, other is...  69 us
    ppermute x28, starting transfers between devices, send(): return lax.ppermute(value, ('grp', 'tok'), flips(first, second))  29.6 us
    all_to_all x1, blocking collectives, carry_scan(): landed = lax.all_to_all(packed, ('grp', 'tok'), 0, 0, tiled=True)  23.5 us
    all_to_all x1, waiting for transfers between devices, reduce_vectors(): landed = lax.all_to_all(spread, ('grp', 'tok'), 0, 0, tiled=True)  23.5 us
    unnamed x41, local copies, waits for them, and re-layouts  10.9 us
    pallas_call x2, Pallas kernels, carry_scan(): pl.pallas_call(partial(chain_kernel, backward), out_shape=shape_of(landed...  10.2 us
  transfers between devices with their start and end apart: 32, of which 13 were waited for; matrix products, arithmetic and copies ran while one was open for 8% of the time, Pallas kernels for 33%

commit v1 on v0

v1 whole, which is shorter than its diff:
```python
from functools import partial

import jax
import jax.numpy as jnp
from jax import lax
from jax.experimental import pallas as pl
from jax.experimental.pallas import tpu as pltpu
from jax.sharding import PartitionSpec as P


eps = 1e-05
f32 = jnp.float32
bf16 = jnp.bfloat16
grant = 58 * 1024 * 1024


def dg(left, right, left_dim, right_dim):
    dims = (((left_dim,), (right_dim,)), ((), ()))
    return lax.dot_general(left, right, dims, preferred_element_type=f32)


def parts_of(value):
    high = value.astype(bf16).astype(f32)
    return high, value - high


def rows_of(rows, width):
    at = lax.broadcasted_iota(jnp.int32, (16, width), 0)
    block = jnp.zeros((16, width), f32)
    for place, row in enumerate(rows):
        block = jnp.where(at == place, row, block)
    return block


def stacked(*blocks):
    return jnp.concatenate([block.astype(bf16) for block in blocks], axis=0)


def norm_parts(value):
    centered = value - jnp.mean(value, axis=1, keepdims=True)
    variance = jnp.mean(centered * centered, axis=1, keepdims=True)
    scale = lax.rsqrt(variance + eps)
    return centered * scale, scale


def norm_back(unit, scale, gain, grad):
    scaled = grad * gain
    along = jnp.mean(scaled * unit, axis=1, keepdims=True)
    return scale * (scaled - jnp.mean(scaled, axis=1, keepdims=True) - unit * along)


def enter_kernel(
    x_ref, gains_ref, w_ref, fq_ref, fk_ref, tail_ref,
    hid_ref, qkv_ref, pq_ref, pk_ref, state_ref, norm_ref, logit_ref,
):
    head_dim, width = fq_ref.shape
    rows = x_ref.shape[0]
    unit, _ = norm_parts(x_ref[...].astype(f32))
    hid = (unit * gains_ref[0:1, :] + gains_ref[1:2, :]).astype(bf16)
    hid_ref[...] = hid.T
    for low in range(0, 3 * width, width):
        qkv_ref[low : low + width, :] = dg(hid, w_ref[:, low : low + width], 1, 0).astype(bf16).T

    @pl.when(pl.program_id(0) == 0)
    def _():
        state_ref[...] = jnp.zeros_like(state_ref)
        norm_ref[...] = jnp.zeros_like(norm_ref)

    heads = width // head_dim
    for low in range(0, width, head_dim):
        high = low + head_dim
        logit_ref[low:high, :] = dg(fq_ref[:, low:high], qkv_ref[low:high, :], 1, 0)
        logit_ref[width + low : width + high, :] = dg(
            fk_ref[:, low:high], qkv_ref[width + low : width + high, :], 1, 0
        )
    step = min(128, rows)
    for part, phi_ref in enumerate((pq_ref, pk_ref)):
        for low in range(0, width, head_dim):
            first = part * width + low
            for lane in range(0, rows, step):
                lanes = slice(lane, lane + step)
                logits = logit_ref[first : first + head_dim, lanes]
                up = jnp.exp(logits - jnp.max(logits, axis=0, keepdims=True))
                low_most = jnp.exp(jnp.min(logits, axis=0, keepdims=True) - logits)
                up = up * (1.0 / jnp.sum(up, axis=0, keepdims=True))
                low_most = low_most * (1.0 / jnp.sum(low_most, axis=0, keepdims=True))
                phi_ref[2 * low : 2 * low + head_dim, lanes] = up.astype(bf16)
                phi_ref[2 * low + head_dim : 2 * low + 2 * head_dim, lanes] = low_most.astype(bf16)
    ones = jnp.ones((16, rows), bf16)
    for head in range(heads):
        low, high = (head * head_dim, (head + 1) * head_dim)
        wide = stacked(qkv_ref[2 * width + low : 2 * width + high, :], ones)
        local = dg(wide, pk_ref[2 * low : 2 * high, :] * tail_ref[...], 1, 1)
        state_ref[low:high, :] += local[:head_dim]
        norm_ref[head : head + 1, :] += local[head_dim : head_dim + 1]


def masked(scores, start, first, offset):
    key_at = lax.broadcasted_iota(jnp.int32, scores.shape, 0) + first
    allowed = key_at >= start
    if first + scores.shape[0] > offset:
        query_at = lax.broadcasted_iota(jnp.int32, scores.shape, 1) + offset
        allowed = allowed & (key_at <= query_at)
    return jnp.where(allowed, scores, 0.0).astype(bf16)


def causal(make, start, low, high):
    blocks = [masked(make(0, low), start, 0, low)] if low else []
    return jnp.concatenate(blocks + [masked(make(low, high), start, low, low)], axis=0)


def local_kernel(pq_ref, pk_ref, v_ref, start_ref, num_ref, den_ref):
    tokens = pq_ref.shape[1]
    head_dim = v_ref.shape[0]
    step = min(256, tokens)
    lows = list(range(0, tokens, step))

    def weights_at(low):
        phi = pq_ref[:, low : low + step]
        make = lambda first, last: dg(pk_ref[:, first:last], phi, 0, 0)
        return causal(make, start_ref[:, low : low + step], low, low + step)

    upcoming = weights_at(lows[-1])
    for at in range(len(lows) - 1, -1, -1):
        weights = upcoming
        low, high = (lows[at], lows[at] + step)
        if at:
            upcoming = weights_at(lows[at - 1])
        wide = stacked(v_ref[:, :high], jnp.ones((16, high), bf16))
        local = dg(wide, weights, 1, 0)
        num_ref[:, low:high] = local[:head_dim]
        den_ref[0, :, low:high] = local[head_dim : head_dim + 1]


def block_kernel(
    num0_ref, num1_ref, den0_ref, den1_ref, pq_ref, state_ref, norm_ref, open_ref, x_ref, cot_ref, gains_ref,
    wout_ref, wfc_ref, wproj_ref,
    low_ref, hid_ref, act_ref, dpre_ref, out_ref, dbranch_ref, dresid_ref, dnum_ref, dden_ref,
    gstate_ref, gnorm_ref, sums_ref,
    mixed_ref, inverse_ref,
):
    width, features = state_ref.shape
    head_dim = features // 2
    rows = x_ref.shape[0]
    opened = open_ref[...]

    @pl.when(pl.program_id(0) == 0)
    def _():
        gstate_ref[...] = jnp.zeros_like(gstate_ref)
        gnorm_ref[...] = jnp.zeros_like(gnorm_ref)
        sums_ref[...] = jnp.zeros_like(sums_ref)

    for head in range(width // head_dim):
        low, high = (head * head_dim, (head + 1) * head_dim)
        state = parts_of(state_ref[low:high, :])
        normer = rows_of(parts_of(norm_ref[head : head + 1, :]), features)
        carry = dg(stacked(*state, normer), pq_ref[2 * low : 2 * high, :], 1, 0)
        half = width // 2
        num_ref, den_ref = (num0_ref, den0_ref) if low < half else (num1_ref, den1_ref)
        num = num_ref[low % half : low % half + head_dim, :]
        num = num + opened * (carry[:head_dim] + carry[head_dim:features])
        den = den_ref[head % (half // head_dim)]
        den = den + opened * (carry[features : features + 1] + carry[features + 1 : features + 2])
        inverse = 1.0 / den
        mixed = num * inverse
        inverse_ref[head : head + 1, :] = inverse
        mixed_ref[low:high, :] = mixed
        low_ref[low:high, :] = mixed.astype(bf16)
    resid = x_ref[...].astype(f32) + dg(low_ref[...], wout_ref[...], 0, 0)
    unit, scale = norm_parts(resid)
    hid = (unit * gains_ref[2:3, :] + gains_ref[3:4, :]).astype(bf16)
    hid_ref[...] = hid.T
    cot = cot_ref[...]
    hidden = wfc_ref.shape[1]
    step = hidden // 4
    root = 0.7978845608028654

    def entering(low):
        pre = dg(hid, wfc_ref[:, low : low + step], 1, 0)
        return pre, dg(cot, wproj_ref[low : low + step, :], 1, 1)

    upcoming = entering(0)
    out, dhid = (resid, None)
    for low in range(0, hidden, step):
        pre, dact = upcoming
        if low + step < hidden:
            upcoming = entering(low + step)
        square = pre * pre
        half = 0.5 + 0.5 * jnp.tanh(pre * (root + (root * 0.044715) * square))
        act = pre * half
        rise = (1.0 - half) * (2.0 * root + (6.0 * root * 0.044715) * square)
        dpre = (dact * (half + act * rise)).astype(bf16)
        act = act.astype(bf16)
        act_ref[:, low : low + step] = act
        dpre_ref[:, low : low + step] = dpre
        out = out + dg(act, wproj_ref[low : low + step, :], 1, 0)
        local = dg(dpre, wfc_ref[:, low : low + step], 1, 1)
        dhid = local if dhid is None else dhid + local
    out_ref[...] = out.astype(bf16)
    sums_ref[0:1, :] += jnp.sum(dhid * unit, axis=0, keepdims=True)
    sums_ref[1:2, :] += jnp.sum(dhid, axis=0, keepdims=True)
    dresid = cot.astype(f32) + norm_back(unit, scale, gains_ref[2:3, :], dhid)
    dresid_ref[...] = dresid
    dbranch = dresid.astype(bf16)
    dbranch_ref[...] = dbranch
    dmixed_all = dg(wout_ref[...], dbranch, 1, 1)
    for head in range(width // head_dim):
        low, high = (head * head_dim, (head + 1) * head_dim)
        dmixed = dmixed_all[low:high]
        inverse = inverse_ref[head : head + 1, :]
        dnum = dmixed * inverse
        dden = -jnp.sum(dmixed * mixed_ref[low:high, :], axis=0, keepdims=True) * inverse
        dnum_ref[low:high, :] = dnum
        dden_ref[head] = dden
        wide = stacked(*parts_of(dnum * opened), rows_of(parts_of(dden * opened), rows))
        local = dg(wide, pq_ref[2 * low : 2 * high, :], 1, 1)
        gstate_ref[low:high, :] += local[:head_dim] + local[head_dim:features]
        gnorm_ref[head : head + 1, :] += local[features : features + 1] + local[features + 1 : features + 2]


def logit_back(phi, dphi):
    half = phi.shape[0] // 2
    up, down = (phi[:half].astype(f32), phi[half:].astype(f32))
    dup, ddown = (dphi[:half], dphi[half:])
    dup = dup - jnp.sum(dup * up, axis=0, keepdims=True)
    ddown = ddown - jnp.sum(ddown * down, axis=0, keepdims=True)
    return (up * dup - down * ddown).astype(bf16)


def local_back_kernel(
    pq_ref, pk_ref, q_ref, v_ref, dnum_ref, dden_ref, start_ref, open_ref, state_ref, norm_ref, fq_ref,
    dq_ref, gfq_ref, dphik_ref, dv_ref,
):
    tokens = pq_ref.shape[1]
    features = pq_ref.shape[0]
    step = min(256, tokens)
    state_high, state_low = parts_of(state_ref[...])
    norm_high, norm_low = parts_of(norm_ref[0])
    carried = stacked(
        state_high, state_high, state_low, rows_of((norm_high, norm_high, norm_low), features)
    )
    maps = fq_ref[...]
    gfq = jnp.zeros(gfq_ref.shape[1:], f32)
    lows = list(range(0, tokens, step))

    def weights_at(low):
        high = low + step
        start = start_ref[:, low:high]
        phi = pq_ref[:, low:high]
        dnum_low = dnum_ref[:, low:high].astype(bf16)
        dden = dden_ref[0, :, low:high]
        plain = lambda first, last: dg(pk_ref[:, first:last], phi, 0, 0)
        slope = lambda first, last: dg(v_ref[:, first:last], dnum_low, 0, 0) + dden
        return causal(plain, start, low, high), causal(slope, start, low, high)

    upcoming = weights_at(lows[-1])
    for at in range(len(lows) - 1, -1, -1):
        low, high = (lows[at], lows[at] + step)
        weights, dweights = upcoming
        if at:
            upcoming = weights_at(lows[at - 1])
        phi = pq_ref[:, low:high]
        num_high, num_low = parts_of(dnum_ref[:, low:high])
        dden = dden_ref[0, :, low:high]
        dv = dg(num_high.astype(bf16), weights, 1, 1)
        dphik = dg(phi, dweights, 1, 1)
        if at == len(lows) - 1:
            dv_ref[...] = dv
            dphik_ref[...] = dphik
        else:
            dv_ref[:, :high] += dv
            dphik_ref[:, :high] += dphik
        den_high, den_low = parts_of(dden)
        arriving = stacked(num_high, num_low, num_high, rows_of((den_high, den_low, den_high), step))
        dphi = dg(pk_ref[:, :high], dweights, 1, 0)
        dphi = dphi + open_ref[:, low:high] * dg(carried, arriving, 0, 0)
        dlogit = logit_back(phi, dphi)
        gfq = gfq + dg(q_ref[:, low:high], dlogit, 1, 1)
        dq_ref[:, low:high] = dg(maps, dlogit, 1, 0).astype(bf16)
    gfq_ref[0] = gfq


def key_back_kernel(
    pk_ref, k_ref, v_ref, dphik0_ref, dphik1_ref, dv0_ref, dv1_ref, tail_ref, state_ref, norm_ref, fk_ref,
    dkv_ref, gfk_ref,
):
    features, tokens = pk_ref.shape
    head_dim = features // 2
    state_high, state_low = parts_of(state_ref[...])
    carried = stacked(state_high, state_low, rows_of(parts_of(norm_ref[0]), features))
    values = v_ref[...]
    tail = tail_ref[...]
    wide = stacked(values, values, jnp.ones((16, tokens), bf16))
    phi = pk_ref[...]
    early = pl.program_id(0) < pl.num_programs(0) // 2
    dphi = jnp.where(early, dphik0_ref[...], dphik1_ref[...]) + tail * dg(carried, wide, 0, 0)
    both = dg(stacked(state_high, state_low), phi, 1, 0)
    dv = jnp.where(early, dv0_ref[...], dv1_ref[...]) + tail * (both[:head_dim] + both[head_dim:])
    dlogit = logit_back(phi, dphi)
    gfk_ref[0] = dg(k_ref[...], dlogit, 1, 1)
    dkv_ref[0] = dg(fk_ref[...], dlogit, 1, 0).astype(bf16)
    dkv_ref[1] = dv.astype(bf16)


def leave_kernel(dq0_ref, dq1_ref, dkv_ref, w_ref, x_ref, gains_ref, dresid_ref, grad_ref, sums_ref):
    width = x_ref.shape[1]

    @pl.when(pl.program_id(0) == 0)
    def _():
        sums_ref[...] = jnp.zeros_like(sums_ref)

    dq = jnp.concatenate([dq0_ref[...], dq1_ref[...]], axis=0)
    dhid = dg(dq, w_ref[:, :width], 0, 1)
    dhid = dhid + dg(dkv_ref[0], w_ref[:, width : 2 * width], 0, 1)
    dhid = dhid + dg(dkv_ref[1], w_ref[:, 2 * width :], 0, 1)
    unit, scale = norm_parts(x_ref[...].astype(f32))
    sums_ref[0:1, :] += jnp.sum(dhid * unit, axis=0, keepdims=True)
    sums_ref[1:2, :] += jnp.sum(dhid, axis=0, keepdims=True)
    grad_ref[...] = dresid_ref[...] + norm_back(unit, scale, gains_ref[0:1, :], dhid)


def whole(shape):
    return pl.BlockSpec(shape, lambda i: (0,) * len(shape))


def down(rows, width):
    return pl.BlockSpec((rows, width), lambda i: (i, 0))


def across(rows, width):
    return pl.BlockSpec((rows, width), lambda i: (0, i))


def heads_across(heads, width):
    return pl.BlockSpec((heads, 1, width), lambda i: (0, 0, i))


def one_head(width, first=0):
    return pl.BlockSpec((1, 1, width), lambda i: (first + i, 0, 0))


def head_rows(rows, width, first=0):
    return pl.BlockSpec((rows, width), lambda i: (first + i, 0))


def shape_of(shape, dtype):
    return jax.ShapeDtypeStruct(shape, dtype)


def call(kernel, grid, ins, outs, shapes, args, scratch=()):
    return pl.pallas_call(
        kernel,
        grid=(grid,),
        in_specs=ins,
        out_specs=outs,
        out_shape=shapes,
        scratch_shapes=list(scratch),
        compiler_params=pltpu.CompilerParams(
            dimension_semantics=("arbitrary",), vmem_limit_bytes=grant
        ),
    )(*args)


def log2_of(count):
    return count.bit_length() - 1


def sizes():
    return (lax.axis_size("grp"), lax.axis_size("tok"))


def place_of():
    return lax.axis_index("grp") * lax.axis_size("tok") + lax.axis_index("tok")


def flips(first, second):
    grp_size, tok_size = sizes()
    pairs = []
    for place in range(grp_size * tok_size):
        pairs.append((place, place ^ (second if (place // tok_size) % 2 else first)))
    return pairs


def far_flips():
    grp_size, tok_size = sizes()
    return [(2 * tok_size) << bit for bit in range(log2_of(grp_size) - 1)]


def order_of(turn):
    tok_bits = [1 << bit for bit in range(log2_of(lax.axis_size("tok")))]
    near = far_flips() + tok_bits[:-1]
    turn = turn % len(near)
    return near[turn:] + near[:turn] + tok_bits[-1:]


def slots_of(turn):
    grp_size, tok_size = sizes()
    order = order_of(turn)
    slots = []
    for tok in range(tok_size):
        for far in range(grp_size // 2):
            place = far * 2 * tok_size + tok
            bits = [(place // flip) % 2 for flip in order]
            slots.append(sum(bit << (len(bits) - 1 - at) for at, bit in enumerate(bits)))
    return jnp.array(slots, jnp.int32)


def tables_of(turns):
    core = lax.axis_index("grp") % 2
    own = lax.axis_index("tok") * (lax.axis_size("grp") // 2) + lax.axis_index("grp") // 2
    even, odd = (slots_of(turns[0]), slots_of(turns[1]))
    mine = jnp.where(core == 0, even, odd)
    theirs = jnp.where(core == 0, odd, even)
    return jnp.concatenate([theirs ^ theirs[own], mine ^ mine[own], core[None].astype(jnp.int32)])


def product_kernel(counts, theirs, mine, by_columns, table_ref, *refs):
    count, tails = counts
    ins, refs = (refs[:count], refs[count:])
    tail_refs, refs = (refs[:tails], refs[tails:])
    theirs_ref, keep_ref, give_ref = refs
    pieces = (table_ref.shape[0] - 1) // 2
    half = pieces // 2
    rows, lanes = theirs_ref.shape[1:]
    for turn, forms in enumerate((theirs, mine)):
        at = 0
        blocks = []
        for left, right, left_dim, right_dim in forms:
            right = ins[right][...]
            value = dg(ins[left][...], right.reshape(right.shape[-2:]), left_dim, right_dim)
            blocks.append((at, value))
            at += value.shape[1]
        if tails:
            blocks.append((at, tail_refs[turn][0]))
        base = turn * pieces
        cuts = []
        for column, value in blocks:
            if by_columns:
                far = value.shape[0] // rows
                for tok in range(value.shape[1] // lanes):
                    for place in range(far):
                        part = value[place * rows : (place + 1) * rows, tok * lanes : (tok + 1) * lanes]
                        cuts.append((tok * far + place, slice(0, lanes), part))
                base = turn * pieces + pl.program_id(0) * len(cuts)
            else:
                for piece in range(value.shape[0] // rows):
                    part = value[piece * rows : (piece + 1) * rows]
                    cuts.append((piece, slice(column, column + value.shape[1]), part))
        for piece, span, part in cuts:
            slot = table_ref[base + piece]
            if turn == 0:
                theirs_ref[slot, :, span] = part
                continue

            @pl.when(slot < half)
            def _(part=part, span=span, slot=slot):
                keep_ref[slot, :, span] = part

            @pl.when(slot >= half)
            def _(part=part, span=span, slot=slot):
                give_ref[slot - half, :, span] = part


def products(table, theirs, mine, ins, specs, grid, piece, tail=None, by_columns=False):
    pieces = (table.shape[0] - 1) // 2
    if by_columns or grid == 1:
        block = lambda count: pl.BlockSpec((count,) + piece, lambda i, t: (0, 0, 0))
    else:
        block = lambda count: pl.BlockSpec((count, piece[0], piece[1] // grid), lambda i, t: (0, 0, i))
    specs = list(specs)
    ins = list(ins)
    count = len(ins)
    if tail is not None:
        ins += [tail, tail]
        specs.append(pl.BlockSpec((1,) + tail.shape[1:], lambda i, t: (1 - t[2 * pieces], 0, 0)))
        specs.append(pl.BlockSpec((1,) + tail.shape[1:], lambda i, t: (t[2 * pieces], 0, 0)))
    counts = (pieces, pieces // 2, pieces // 2)
    return pl.pallas_call(
        partial(product_kernel, (count, len(ins) - count), theirs, mine, by_columns),
        grid_spec=pltpu.PrefetchScalarGridSpec(
            num_scalar_prefetch=1, grid=(grid,), in_specs=specs, out_specs=[block(c) for c in counts]
        ),
        out_shape=[shape_of((c,) + piece, f32) for c in counts],
        compiler_params=pltpu.CompilerParams(
            dimension_semantics=("arbitrary",), vmem_limit_bytes=grant
        ),
    )(table, *ins)


def send(value, first, second):
    return lax.ppermute(value, ("grp", "tok"), flips(first, second))


def swap_cores(value):
    tok_size = lax.axis_size("tok")
    return send(value, tok_size, tok_size)


def fold(keep, give, other, turns):
    orders = (order_of(turns[0]), order_of(turns[1]))
    count = keep.shape[0]
    give = give + other[count:]
    other = other[:count]
    for at, (even, odd) in enumerate(zip(*orders)):
        landed = send(give, even, odd)
        half = keep.shape[0] // 2
        if at == 0:
            landed_of = lambda low, high: landed[low:high] + other[low:high]
        else:
            landed_of = lambda low, high: landed[low:high]
        if half:
            give = keep[half:] + landed_of(half, 2 * half)
            keep = keep[:half] + landed_of(0, half)
        else:
            keep = keep + landed_of(0, 1)
    for flip in far_flips():
        bit = (place_of() & flip) != 0
        landed = send(keep, flip, flip)
        keep = jnp.concatenate(
            [jnp.where(bit, landed, keep), jnp.where(bit, keep, landed)], axis=0
        )
    keep = keep.reshape(-1, keep.shape[2])
    landed = swap_cores(keep)
    core = lax.axis_index("grp") % 2
    return (jnp.where(core == 0, keep, landed), jnp.where(core == 0, landed, keep))


def chain_kernel(backward, got_ref, out_ref):
    count, rows, lanes = got_ref.shape

    def step(at, so_far):
        block = count - 1 - at if backward else at
        out_ref[block] = so_far
        local = got_ref[block]
        return local + local[rows - 1 :, lanes - 1 :] * so_far

    lax.fori_loop(0, count, step, jnp.zeros((rows, lanes), f32), unroll=8)


def carry_scan(state, norm, keep, backward):
    grp_size, tok_size = sizes()
    count = grp_size * tok_size
    lanes = state.shape[1]
    share = state.shape[0] // count
    spare = norm.size // count
    extra = jnp.concatenate(
        [norm.reshape(count, spare), jnp.zeros((count, lanes - 1 - spare), f32), jnp.full((count, 1), keep)],
        axis=1,
    )
    packed = jnp.concatenate([state.reshape(count, share, lanes), extra[:, None]], axis=1)
    landed = lax.all_to_all(packed, ("grp", "tok"), 0, 0, tiled=True)
    summed = pl.pallas_call(
        partial(chain_kernel, backward),
        out_shape=shape_of(landed.shape, f32),
        compiler_params=pltpu.CompilerParams(vmem_limit_bytes=grant),
    )(landed)
    home = lax.all_to_all(summed, ("grp", "tok"), 0, 0, tiled=True)
    return home[:, :share].reshape(state.shape), home[:, share, :spare].reshape(norm.shape)


def reduce_vectors(stack):
    grp_size, tok_size = sizes()
    count, length = stack.shape
    share = length // tok_size
    blocks = stack.reshape(count, tok_size, share).transpose(1, 0, 2)
    blocks = blocks.reshape(tok_size, count * share)
    spread = jnp.broadcast_to(blocks[None], (grp_size,) + blocks.shape)
    spread = spread.reshape(grp_size * tok_size, count * share)
    landed = lax.all_to_all(spread, ("grp", "tok"), 0, 0, tiled=True)
    return jnp.sum(landed, axis=0).reshape(count, share)


def on_device(
    layer_input,
    doc_starts,
    ln1_gain,
    ln1_shift,
    w_qkv,
    feat_q,
    feat_k,
    w_out,
    ln2_gain,
    ln2_shift,
    w_fc,
    w_proj,
    cotangent,
):
    tokens, width = layer_input.shape
    head_dim = feat_q.shape[1]
    heads = width // head_dim
    feats = 2 * head_dim
    hidden = w_fc.shape[1]
    rows = min(256, tokens)
    blocks = tokens // rows
    gains = jnp.stack([ln1_gain, ln1_shift, ln2_gain, ln2_shift])

    at = jnp.arange(tokens, dtype=jnp.int32)
    marked = (doc_starts[:, None] > 0) & (at[:, None] <= at[None, :])
    last = jnp.max(jnp.where(marked, at[:, None], -1), axis=0)
    start = jnp.maximum(last, 0)[None]
    opened = (last < 0).astype(f32)[None]
    tail = (at >= last[-1]).astype(f32)[None]
    keep = (last[-1] < 0).astype(f32)

    hid1, qkv, phi_q, phi_k, state, norm = call(
        enter_kernel, blocks,
        [down(rows, width), whole((4, width)), whole(w_qkv.shape),
         whole((head_dim, width)), whole((head_dim, width)), across(1, rows)],
        [across(width, rows), across(3 * width, rows), across(2 * width, rows), across(2 * width, rows),
         whole((width, feats)), whole((heads, feats))],
        [shape_of((width, tokens), bf16), shape_of((3 * width, tokens), bf16),
         shape_of((2 * width, tokens), bf16), shape_of((2 * width, tokens), bf16),
         shape_of((width, feats), f32), shape_of((heads, feats), f32)],
        (layer_input, gains, w_qkv, feat_q.T, feat_k.T, tail.astype(bf16)),
        [pltpu.VMEM((2 * width, rows), f32)],
    )
    state_in, norm_in = carry_scan(state, norm, keep, False)
    part = heads // 2
    locals_ = [
        call(
            local_kernel, part,
            [head_rows(feats, tokens, at * part), head_rows(feats, tokens, at * part),
             head_rows(head_dim, tokens, 2 * heads + at * part), whole((1, tokens))],
            [head_rows(head_dim, tokens), one_head(tokens)],
            [shape_of((width // 2, tokens), f32), shape_of((part, 1, tokens), f32)],
            (phi_q, phi_k, qkv, start),
        )
        for at in range(2)
    ]
    once = lambda shape: pl.BlockSpec(shape, lambda i: (0, 0), pipeline_mode=pl.Buffered(1))
    mixed_low, hid2, act, dpre, output, dbranch, dresid, dnum, dden, back_state, back_norm, sums2 = call(
        block_kernel, blocks,
        [across(width // 2, rows), across(width // 2, rows), heads_across(part, rows),
         heads_across(part, rows), across(2 * width, rows), whole((width, feats)),
         whole((heads, feats)), across(1, rows), down(rows, width), down(rows, width), whole((4, width)),
         once(w_out.shape), once(w_fc.shape), once(w_proj.shape)],
        [across(width, rows), across(width, rows), down(rows, hidden), down(rows, hidden),
         down(rows, width), down(rows, width), down(rows, width), across(width, rows),
         heads_across(heads, rows), whole((width, feats)), whole((heads, feats)), whole((8, width))],
        [shape_of((width, tokens), bf16), shape_of((width, tokens), bf16), shape_of((tokens, hidden), bf16),
         shape_of((tokens, hidden), bf16), shape_of((tokens, width), bf16), shape_of((tokens, width), bf16),
         shape_of((tokens, width), f32), shape_of((width, tokens), f32), shape_of((heads, 1, tokens), f32),
         shape_of((width, feats), f32), shape_of((heads, feats), f32), shape_of((8, width), f32)],
        (locals_[0][0], locals_[1][0], locals_[0][1], locals_[1][1], phi_q, state_in, norm_in, opened,
         layer_input, cotangent, gains, w_out, w_fc, w_proj),
        [pltpu.VMEM((width, rows), f32), pltpu.VMEM((16, rows), f32)],
    )
    half = width // 2
    fars, toks = (lax.axis_size("grp") // 2, lax.axis_size("tok"))
    piece_rows = width // (fars * toks)
    turns_a, turns_b, turns_c, turns_d = ((0, 1), (2, 0), (1, 2), (0, 1))
    table_a, table_b, table_c, table_d = map(tables_of, (turns_a, turns_b, turns_c, turns_d))
    last_at = table_a.shape[0] - 1
    plain = lambda rows_: pl.BlockSpec((rows_, tokens), lambda i, t: (0, 0))
    which = lambda turn, t: t[last_at] if turn else 1 - t[last_at]
    right_half = lambda turn: pl.BlockSpec((tokens, half), lambda i, t: (0, which(turn, t)))
    chosen = lambda row, turn: pl.BlockSpec((1, half, tokens), lambda i, t: (row, which(turn, t), 0))
    quarter = lambda turn: pl.BlockSpec((tokens, hidden // 8), lambda i, t: (0, 4 * which(turn, t) + i))
    theirs_a, keep_a, give_a = products(
        table_a, ((0, 2, 0, 0),), ((1, 2, 0, 0),), (cotangent, cotangent, act),
        (right_half(0), right_half(1), pl.BlockSpec((tokens, hidden // 4), lambda i, t: (0, i))),
        4, (half // fars, hidden // toks), None, True,
    )
    other_a = swap_cores(theirs_a)
    theirs_b, keep_b, give_b = products(
        table_b, ((0, 1, 1, 0),), ((0, 2, 1, 0),), (hid2, dpre, dpre),
        (plain(width), quarter(0), quarter(1)), 4, (piece_rows, hidden // 2),
    )
    other_b = swap_cores(theirs_b)
    state_back, norm_back_in = carry_scan(back_state, back_norm, keep, True)
    split = [
        call(
            local_back_kernel, part,
            [head_rows(feats, tokens, at * part), head_rows(feats, tokens, at * part),
             head_rows(head_dim, tokens, at * part), head_rows(head_dim, tokens, 2 * heads + at * part),
             head_rows(head_dim, tokens, at * part), one_head(tokens, at * part),
             whole((1, tokens)), whole((1, tokens)), head_rows(head_dim, feats, at * part),
             one_head(feats, at * part), head_rows(head_dim, head_dim, at * part)],
            [head_rows(head_dim, tokens), pl.BlockSpec((1, head_dim, head_dim), lambda i: (i, 0, 0)),
             head_rows(feats, tokens), head_rows(head_dim, tokens)],
            [shape_of((width // 2, tokens), bf16), shape_of((part, head_dim, head_dim), f32),
             shape_of((width, tokens), f32), shape_of((width // 2, tokens), f32)],
            (phi_q, phi_k, qkv, qkv, dnum, dden, start, opened, state_in, norm_in[:, None], feat_q),
        )
        for at in range(2)
    ]
    gfq = jnp.concatenate([split[0][1], split[1][1]], axis=0)
    lower = lambda rows_: pl.BlockSpec((rows_, tokens), lambda i: (jnp.minimum(i, part - 1), 0))
    upper = lambda rows_: pl.BlockSpec((rows_, tokens), lambda i: (jnp.maximum(i - part, 0), 0))
    dkv, gfk = call(
        key_back_kernel, heads,
        [head_rows(feats, tokens), head_rows(head_dim, tokens, heads),
         head_rows(head_dim, tokens, 2 * heads), lower(feats), upper(feats), lower(head_dim), upper(head_dim),
         whole((1, tokens)), head_rows(head_dim, feats), one_head(feats), head_rows(head_dim, head_dim)],
        [pl.BlockSpec((2, head_dim, tokens), lambda i: (0, i, 0)),
         pl.BlockSpec((1, head_dim, head_dim), lambda i: (i, 0, 0))],
        [shape_of((2, width, tokens), bf16), shape_of((heads, head_dim, head_dim), f32)],
        (phi_k, qkv, qkv, split[0][2], split[1][2], split[0][3], split[1][3], tail, state_back, norm_back_in[:, None], feat_k),
    )
    grad_input, sums1 = call(
        leave_kernel, blocks,
        [across(width // 2, rows), across(width // 2, rows),
         pl.BlockSpec((2, width, rows), lambda i: (0, 0, i)), whole(w_qkv.shape),
         down(rows, width), whole((4, width)), down(rows, width)],
        [down(rows, width), whole((8, width))],
        [shape_of((tokens, width), f32), shape_of((8, width), f32)],
        (split[0][0], split[1][0], dkv, w_qkv, layer_input, gains, dresid),
    )

    first_core = lax.axis_index("grp") % 2 == 0
    theirs_q = jnp.where(first_core, split[1][0], split[0][0])
    mine_q = jnp.where(first_core, split[0][0], split[1][0])
    theirs_c, keep_c, give_c = products(
        table_c, ((0, 1, 1, 0), (3, 4, 1, 1)), ((0, 2, 1, 0), (3, 5, 1, 1)),
        (mixed_low, dbranch, dbranch, hid1, theirs_q, mine_q),
        (plain(width), right_half(0), right_half(1), plain(width), plain(half), plain(half)),
        1, (piece_rows, 2 * half),
    )
    other_c = swap_cores(theirs_c)
    feats_both = jnp.stack([gfq.reshape(width, head_dim), gfk.reshape(width, head_dim)])
    feats_both = jnp.pad(feats_both, ((0, 0), (0, 0), (0, feats - head_dim)))

    theirs_d, keep_d, give_d = products(
        table_d, ((0, 1, 1, 1), (0, 2, 1, 1)), ((0, 3, 1, 1), (0, 4, 1, 1)),
        (hid1, dkv, dkv, dkv, dkv),
        (plain(width), chosen(0, 0), chosen(1, 0), chosen(0, 1), chosen(1, 1)),
        1, (piece_rows, 2 * half + feats), feats_both,
    )
    other_d = swap_cores(theirs_d)
    vectors = reduce_vectors(jnp.concatenate([sums1[:2], sums2[:2]], axis=0))
    grad_proj = jnp.concatenate(fold(keep_a, give_a, other_a, turns_a), axis=0).T
    grad_fc = jnp.concatenate(fold(keep_b, give_b, other_b, turns_b), axis=1)
    c_pair = fold(keep_c, give_c, other_c, turns_c)
    d_pair = fold(keep_d, give_d, other_d, turns_d)
    grad_out = jnp.concatenate([part[:, :half] for part in c_pair], axis=1)
    grad_qkv = jnp.concatenate(
        [part[:, half:] for part in c_pair]
        + [part[:, :half] for part in d_pair]
        + [part[:, half : 2 * half] for part in d_pair],
        axis=1,
    )
    return (
        output,
        grad_input,
        vectors[0],
        vectors[1],
        grad_qkv,
        d_pair[0][:, 2 * half : 2 * half + head_dim],
        d_pair[1][:, 2 * half : 2 * half + head_dim],
        grad_out,
        vectors[2],
        vectors[3],
        grad_fc,
        grad_proj,
    )


def solution(mesh):
    in_specs = (
        P(("grp", "tok"), None),
        P(("grp", "tok")),
        P(),
        P(),
        P(),
        P(),
        P(),
        P(),
        P(),
        P(),
        P(),
        P(),
        P(("grp", "tok"), None),
    )
    out_specs = (
        P(("grp", "tok"), None),
        P(("grp", "tok"), None),
        P("tok"),
        P("tok"),
        P("tok", None),
        P("tok", None),
        P("tok", None),
        P("tok", None),
        P("tok"),
        P("tok"),
        P("tok", None),
        P("tok", None),
    )

    return jax.shard_map(on_device, mesh=mesh, in_specs=in_specs, out_specs=out_specs, check_vma=False)
```

time: 497 us -> 468 us (0.942)
  Pallas kernels: 247 us -> 175 us
  waiting for transfers between devices: 113 us -> 160 us
  other arithmetic: 33.7 us -> 45.3 us
  starting transfers between devices: 46.8 us -> 36.5 us
    pallas_call x11 -> x8, Pallas kernels: 168 us -> 126 us  [call(): pl.pallas_call(kernel, grid=(grid,), in_specs=ins, out_specs=outs, out_sh...]
    pallas_call x8 -> x4, Pallas kernels: 69 us -> 44.6 us  [products(): pl.pallas_call(partial(product_kernel, (count, len(ins) - count), theirs,...]
    ppermute x28, waiting for transfers between devices: 89.8 us -> 111 us  [send(): return lax.ppermute(value, ('grp', 'tok'), flips(first, second))]
    all_to_all x1, waiting for transfers between devices: 23.5 us -> 41.8 us  [reduce_vectors(): landed = lax.all_to_all(spread, ('grp', 'tok'), 0, 0, tiled=True)]
    add x16 -> x20, other arithmetic: 11.5 us -> 25.1 us  [the longest x4 10.3 us: fold(): give = give + other[count:]]
    ppermute x28, starting transfers between devices: 29.6 us -> 22.8 us  [send(): return lax.ppermute(value, ('grp', 'tok'), flips(first, second))]
    pallas_call x2, Pallas kernels: 10.2 us -> 4.63 us  [carry_scan(): pl.pallas_call(partial(chain_kernel, backward), out_shape=shape_of(landed...]
    all_to_all x1, waiting for transfers between devices: 0.01 us -> 5.17 us  [carry_scan(): landed = lax.all_to_all(packed, ('grp', 'tok'), 0, 0, tiled=True)]
  transfers between devices with their start and end apart: 32 -> 32, of which waited for: 13 -> 16; matrix products, arithmetic and copies ran while one was open for 8% -> 11% of each run, Pallas kernels for 33% -> 19%
where the time goes in v1:
time: 468 us; the launch traced here: 466 us
  Pallas kernels  175 us (37%)
  waiting for transfers between devices  160 us (34%)
  other arithmetic  45.3 us (10%)
  starting transfers between devices  36.5 us (8%)
  blocking collectives  23.5 us (5%)
  local copies, waits for them, and re-layouts  23.2 us (5%)
    pallas_call x8, Pallas kernels, call(): pl.pallas_call(kernel, grid=(grid,), in_specs=ins, out_specs=outs, out_sh...  126 us
    ppermute x28, waiting for transfers between devices, send(): return lax.ppermute(value, ('grp', 'tok'), flips(first, second))  111 us
    pallas_call x4, Pallas kernels, products(): pl.pallas_call(partial(product_kernel, (count, len(ins) - count), theirs,...  44.6 us
    all_to_all x1, waiting for transfers between devices, reduce_vectors(): landed = lax.all_to_all(spread, ('grp', 'tok'), 0, 0, tiled=True)  41.8 us
    all_to_all x1, blocking collectives, carry_scan(): landed = lax.all_to_all(packed, ('grp', 'tok'), 0, 0, tiled=True)  23.5 us
    ppermute x28, starting transfers between devices, send(): return lax.ppermute(value, ('grp', 'tok'), flips(first, second))  22.8 us
    add x4, other arithmetic, fold(): give = give + other[count:]  10.3 us
    add x8, other arithmetic, fold(): keep = keep[:half] + landed_of(0, half)  10.1 us
  transfers between devices with their start and end apart: 32, of which 16 were waited for; matrix products, arithmetic and copies ran while one was open for 11% of the time, Pallas kernels for 19%

profile of v1, /device:TPU:0, one launch (start us, length us, event | category | flops | bytes accessed | tf_op | source)
XLA Modules:
  0.0 465.5 jit_solution(11911150665012937702)
XLA Ops:
  6.9 14.8 %shard_map.292 = (bf16[768,1024]{1,0:T(8,128)(2,1)}, bf16[2304,1024]{1,0:T(8,128)(2,1)}, bf16[1536,1024]{1,0:T(8,128)(2,1)}, bf16[1536,1024]{1,0:T(8,128)(2,1)}, f32[768,128]{1,0:T(8,128)}, /*index=5*/f32[12,128]{1,0:T(8,128)}) custom-call(bf16[1024,768]{1,0:T(8,128)(2,1)} %x_ref.5, f32[4,768]{1,0:T(4,128)} %pad_maximum_fusion.9.gains_ref, ...), custom_call_target="tpu_custom_call" | custom-call | tf_op jit(solution)/shard_map/pallas_call | solution.py:351
  24.4 23.5 %all_to_all.29.got_ref = f32[32,25,128]{2,1,0:T(8,128)} all-to-all(f32[32,25,128]{2,1,0:T(8,128)S(1)} %pad_maximum_fusion.3), channel_id=1, replica_groups=mesh['grp'=4,'tok'=8] {'grp','tok'}, dimensions={0} | all-to-all | bytes 819200 | tf_op jit(solution)/shard_map/all_to_all | solution.py:551
  50.1 2.8 all-to-all-start.1
  53.5 7.7 %shard_map.294 = (f32[384,1024]{1,0:T(8,128)}, f32[6,1,1024]{2,1,0:T(1,128)}) custom-call(bf16[1536,1024]{1,0:T(8,128)(2,1)} %get-tuple-element.58.pq_ref, bf16[1536,1024]{1,0:T(8,128)(2,1)} %get-tuple-element.59.pk_ref, bf16[2304,1024]{1,0:T(8,128)(2,1)} %get-tuple-element.60.v_ref.q_ref.k_ref, s32[1,1024]{1,0:T(1,128)} %bitcast.55), custom_call_target="tpu_custom_call" | custom-call | tf_op jit(solution)/shard_map/pallas_call | solution.py:351
  61.2 7.7 %shard_map.293 = (f32[384,1024]{1,0:T(8,128)}, f32[6,1,1024]{2,1,0:T(1,128)}) custom-call(bf16[1536,1024]{1,0:T(8,128)(2,1)} %get-tuple-element.58.pq_ref, bf16[1536,1024]{1,0:T(8,128)(2,1)} %get-tuple-element.59.pk_ref, bf16[2304,1024]{1,0:T(8,128)(2,1)} %get-tuple-element.60.v_ref.q_ref.k_ref, s32[1,1024]{1,0:T(1,128)} %bitcast.56), custom_call_target="tpu_custom_call" | custom-call | tf_op jit(solution)/shard_map/pallas_call | solution.py:351
  73.3 3.9 broadcast_xor_fusion.1
  80.5 38.5 %shard_map.296 = (bf16[768,1024]{1,0:T(8,128)(2,1)}, bf16[768,1024]{1,0:T(8,128)(2,1)}, bf16[1024,3072]{1,0:T(8,128)(2,1)}, bf16[1024,3072]{1,0:T(8,128)(2,1)}, ...) custom-call(f32[384,1024]{1,0:T(8,128)} %get-tuple-element.61.num0_r, ...), custom_call_target="tpu_custom_call" | custom-call | tf_op jit(solution)/shard_map/pallas_call | solution.py:351
  119.1 16.6 %shard_map.298 = (bf16[384,1024]{1,0:T(8,128)(2,1)}, f32[6,64,64]{2,1,0:T(8,128)}, f32[768,1024]{1,0:T(8,128)}, f32[384,1024]{1,0:T(8,128)}) custom-call(bf16[1536,1024]{1,0:T(8,128)(2,1)} %get-tuple-element.58.pq_ref, bf16[1536,1024]{1,0:T(8,128)(2,1)} %get-tuple-element.59.pk_ref, bf16[2304,1024]{1,0:T(8,128)(2,1)} %get-tuple-element.60.v_ref.q_ref.k_ref, ...), custom_call_target="tpu_custom_call" | custom-call | tf_op jit(solution)/shard_map/pallas_call | solution.py:351
  135.7 16.8 %shard_map.297 = (bf16[384,1024]{1,0:T(8,128)(2,1)}, f32[6,64,64]{2,1,0:T(8,128)}, f32[768,1024]{1,0:T(8,128)}, f32[384,1024]{1,0:T(8,128)}) custom-call(bf16[1536,1024]{1,0:T(8,128)(2,1)} %get-tuple-element.58.pq_ref, bf16[1536,1024]{1,0:T(8,128)(2,1)} %get-tuple-element.59.pk_ref, bf16[2304,1024]{1,0:T(8,128)(2,1)} %get-tuple-element.60.v_ref.q_ref.k_ref, ...), custom_call_target="tpu_custom_call" | custom-call | tf_op jit(solution)/shard_map/pallas_call | solution.py:351
  153.5 5.7 %all-to-all-start.2 = ((f32[32,25,128]{2,1,0:T(8,128)}), f32[32,25,128]{2,1,0:T(8,128)S(1)}, u32[]{:S(2)}, u32[]{:S(2)}) async-start(f32[32,25,128]{2,1,0:T(8,128)} %pad_maximum_fusion.4), calls=%async_computation.2 | async-start | bytes 1048576 | tf_op jit(solution)/shard_map/all_to_all | solution.py:551
  160.4 9.5 %shard_map.302 = (f32[16,48,768]{2,1,0:T(8,128)}, f32[8,48,768]{2,1,0:T(8,128)}, f32[8,48,768]{2,1,0:T(8,128)}) custom-call(s32[33]{0:T(128)} %get-tuple-element.216.table_ref, bf16[768,1024]{1,0:T(8,128)(2,1)} %get-tuple-element.83.refs_0_, bf16[1024,768]{1,0:T(8,128)(2,1)} %get-tuple-element.84.refs_1_.refs_2_, ...), custom_call_target="tpu_custom_call" | custom-call | tf_op jit(solution)/shard_map/pallas_call | solution.py:478
  170.2 5.2 %all-to-all-done.2.got_ref = f32[32,25,128]{2,1,0:T(8,128)S(1)} async-done(((f32[32,25,128]{2,1,0:T(8,128)}), f32[32,25,128]{2,1,0:T(8,128)S(1)}, u32[]{:S(2)}, u32[]{:S(2)}) %all-to-all-start.2) | async-done | bytes 409632 | tf_op jit(solution)/shard_map/all_to_all | solution.py:551
  181.9 12.4 %shard_map.305 = (f32[16,192,384]{2,1,0:T(8,128)}, f32[8,192,384]{2,1,0:T(8,128)}, f32[8,192,384]{2,1,0:T(8,128)}) custom-call(s32[33]{0:T(128)} %get-tuple-element.217.table_ref, bf16[1024,768]{1,0:T(8,128)(2,1)} %refs_1_.1, bf16[1024,768]{1,0:T(8,128)(2,1)} %refs_1_.1, bf16[1024,3072]{1,0:T(8,128)(2,1)} %get-tuple-element.100.refs_2_), custom_call_target="tpu_custom_call" | custom-call | tf_op jit(solution)/shard_map/pallas_call | solution.py:478
  198.8 14.0 %shard_map.300 = (bf16[2,768,1024]{2,1,0:T(8,128)(2,1)}, f32[12,64,64]{2,1,0:T(8,128)}) custom-call(bf16[1536,1024]{1,0:T(8,128)(2,1)} %get-tuple-element.59.pk_ref, bf16[2304,1024]{1,0:T(8,128)(2,1)} %get-tuple-element.60.v_ref.q_ref.k_ref, bf16[2304,1024]{1,0:T(8,128)(2,1)} %get-tuple-element.60.v_ref.q_ref.k_ref, ...), custom_call_target="tpu_custom_call" | custom-call | tf_op jit(solution)/shard_map/pallas_call | solution.py:351
  214.8 9.8 %shard_map.303 = (f32[16,48,896]{2,1,0:T(8,128)}, f32[8,48,896]{2,1,0:T(8,128)}, f32[8,48,896]{2,1,0:T(8,128)}) custom-call(s32[33]{0:T(128)} %get-tuple-element.217.table_ref, bf16[768,1024]{1,0:T(8,128)(2,1)} %get-tuple-element.85.refs_3_.refs_0_, bf16[2,768,1024]{2,1,0:T(8,128)(2,1)} %get-tuple-element.78.dkv_ref.refs_1_.refs_2_.refs_3_.refs_4_, ...), custom_call_target="tpu_custom_call" | custom-call | tf_op jit(solution)/shard_map/pallas_call | solution.py:478
  225.2 12.9 %shard_map.304 = (f32[16,48,1536]{2,1,0:T(8,128)}, f32[8,48,1536]{2,1,0:T(8,128)}, f32[8,48,1536]{2,1,0:T(8,128)}) custom-call(s32[33]{0:T(128)} %add_add_fusion.2.table_ref, bf16[768,1024]{1,0:T(8,128)(2,1)} %get-tuple-element.95.refs_0_, bf16[1024,3072]{1,0:T(8,128)(2,1)} %get-tuple-element.96.refs_1_.refs_2_, ...), custom_call_target="tpu_custom_call" | custom-call | tf_op jit(solution)/shard_map/pallas_call | solution.py:478
  241.2 15.2 %collective-permute-done.1 = f32[8,48,768]{2,1,0:T(8,128)S(1)} collective-permute-done((f32[8,48,768]{2,1,0:T(8,128)S(1)}, f32[8,48,768]{2,1,0:T(8,128)S(1)}, u32[]{:S(2)}, u32[]{:S(2)}) %collective-permute-start.1) | collective-permute-done | bytes 1179680 | tf_op jit(solution)/shard_map/ppermute | solution.py:491
  262.3 5.6 %collective-permute-done.2 = f32[4,48,768]{2,1,0:T(8,128)S(1)} collective-permute-done((f32[4,48,768]{2,1,0:T(8,128)S(1)}, f32[4,48,768]{2,1,0:T(8,128)S(1)}, u32[]{:S(2)}, u32[]{:S(2)}) %collective-permute-start.2) | collective-permute-done | bytes 589856 | tf_op jit(solution)/shard_map/ppermute | solution.py:491
  268.7 15.4 %collective-permute-done.3 = f32[2,48,768]{2,1,0:T(8,128)S(1)} collective-permute-done((f32[2,48,768]{2,1,0:T(8,128)S(1)}, f32[2,48,768]{2,1,0:T(8,128)S(1)}, u32[]{:S(2)}, u32[]{:S(2)}) %collective-permute-start.3) | collective-permute-done | bytes 294944 | tf_op jit(solution)/shard_map/ppermute | solution.py:491
  287.0 10.1 %shard_map.301 = (f32[1024,768]{1,0:T(8,128)}, f32[8,768]{1,0:T(8,128)}) custom-call(bf16[384,1024]{1,0:T(8,128)(2,1)} %get-tuple-element.70.dq0_ref, bf16[384,1024]{1,0:T(8,128)(2,1)} %get-tuple-element.71.dq1_ref, bf16[2,768,1024]{2,1,0:T(8,128)(2,1)} %get-tuple-element.78.dkv_ref.refs_1_.refs_2_.refs_3_.refs_4_, bf16[768,2304]{1,0:T(8,128)(2,1)} %w_ref.3, ...), custom_call_target="tpu_custom_call" | custom-call | tf_op jit(solution)/shard_map/pallas_call | solution.py:351
  301.1 4.2 slice_add_fusion
  306.9 3.0 fusion.6
  319.2 41.8 %all-to-all-done.4 = f32[32,1,384]{2,1,0:T(1,128)S(1)} async-done(((f32[32,1,384]{2,1,0:T(1,128)}), f32[32,1,384]{2,1,0:T(1,128)S(1)}, u32[]{:S(2)}, u32[]{:S(2)}) %all-to-all-start.4) | async-done | bytes 49184 | tf_op jit(solution)/shard_map/all_to_all | solution.py:569
  364.6 5.1 %collective-permute-done.10 = f32[2,48,896]{2,1,0:T(8,128)S(1)} collective-permute-done((f32[2,48,896]{2,1,0:T(8,128)S(1)}, f32[2,48,896]{2,1,0:T(8,128)S(1)}, u32[]{:S(2)}, u32[]{:S(2)}) %collective-permute-start.10) | collective-permute-done | bytes 344096 | tf_op jit(solution)/shard_map/ppermute | solution.py:491
  370.2 10.0 %collective-permute-done.11 = f32[1,48,896]{2,1,0:T(8,128)S(1)} collective-permute-done((f32[1,48,896]{2,1,0:T(8,128)S(1)}, f32[1,48,896]{2,1,0:T(8,128)S(1)}, u32[]{:S(2)}, u32[]{:S(2)}) %collective-permute-start.11) | collective-permute-done | bytes 172064 | tf_op jit(solution)/shard_map/ppermute | solution.py:491
  380.8 2.8 fusion.2
  391.1 19.7 %collective-permute-done.23 = f32[4,192,384]{2,1,0:T(8,128)S(1)} collective-permute-done((f32[4,192,384]{2,1,0:T(8,128)S(1)}, f32[4,192,384]{2,1,0:T(8,128)S(1)}, u32[]{:S(2)}, u32[]{:S(2)}) %collective-permute-start.23) | collective-permute-done | bytes 1179680 | tf_op jit(solution)/shard_map/ppermute | solution.py:491
  411.8 17.8 %collective-permute-done.24 = f32[2,192,384]{2,1,0:T(8,128)S(1)} collective-permute-done((f32[2,192,384]{2,1,0:T(8,128)S(1)}, f32[2,192,384]{2,1,0:T(8,128)S(1)}, u32[]{:S(2)}, u32[]{:S(2)}) %collective-permute-start.24) | collective-permute-done | bytes 589856 | tf_op jit(solution)/shard_map/ppermute | solution.py:491
  429.8 3.0 collective-permute-start.18
  435.1 13.8 %collective-permute-done.25 = f32[1,192,384]{2,1,0:T(8,128)} collective-permute-done((f32[1,192,384]{2,1,0:T(8,128)S(1)}, f32[1,192,384]{2,1,0:T(8,128)}, u32[]{:S(2)}, u32[]{:S(2)}) %collective-permute-start.25) | collective-permute-done | bytes 294944 | tf_op jit(solution)/shard_map/ppermute | solution.py:491
  454.6 4.3 collective-permute-done.26
  459.4 2.8 collective-permute-done.19
  (199 shorter events, 87.5 us)
Async XLA Ops:
  50.1 28.2 %all-to-all-start.1 = ((f32[32,25,128]{2,1,0:T(8,128)}), f32[32,25,128]{2,1,0:T(8,128)S(1)}, u32[]{:S(2)}, u32[]{:S(2)}) async-start(f32[32,25,128]{2,1,0:T(8,128)} %shard_map.295), calls=%async_computation.1 | async-start | bytes 1048576 | tf_op jit(solution)/shard_map/all_to_all | solution.py:557
  153.5 21.9 %all-to-all-start.2 = ((f32[32,25,128]{2,1,0:T(8,128)}), f32[32,25,128]{2,1,0:T(8,128)S(1)}, u32[]{:S(2)}, u32[]{:S(2)}) async-start(f32[32,25,128]{2,1,0:T(8,128)} %pad_maximum_fusion.4), calls=%async_computation.2 | async-start | bytes 1048576 | tf_op jit(solution)/shard_map/all_to_all | solution.py:551
  170.0 68.7 %collective-permute-start = (f32[16,48,768]{2,1,0:T(8,128)}, f32[16,48,768]{2,1,0:T(8,128)}, u32[]{:S(2)}, u32[]{:S(2)}) collective-permute-start(f32[16,48,768]{2,1,0:T(8,128)} %get-tuple-element.88), channel_id=1, source_target_pairs={{0,8},{1,9},{2,10},{3,11},{4,12},{5,13},{6,14},{7,15},{8,0},{9,1},... | collective-permute-start | bytes 7077896 | tf_op jit(solution)/shard_map/ppermute | solution.py:491
  178.5 18.8 %all-to-all-start.3 = ((f32[32,25,128]{2,1,0:T(8,128)}), f32[32,25,128]{2,1,0:T(8,128)S(1)}, u32[]{:S(2)}, u32[]{:S(2)}) async-start(f32[32,25,128]{2,1,0:T(8,128)} %shard_map.299), calls=%async_computation.3 | async-start | bytes 1048576 | tf_op jit(solution)/shard_map/all_to_all | solution.py:557
  194.3 106.8 %collective-permute-start.21 = (f32[16,192,384]{2,1,0:T(8,128)}, f32[16,192,384]{2,1,0:T(8,128)}, u32[]{:S(2)}, u32[]{:S(2)}) collective-permute-start(f32[16,192,384]{2,1,0:T(8,128)} %get-tuple-element.103), channel_id=1, source_target_pairs={{0,8},{1,9},{2,10},{3,11},{4,12},{5,13},{6,14},{7,15},{8,0},{9,1},... | collective-permute-start | bytes 14155784 | tf_op jit(solution)/shard_map/ppermute | solution.py:491
  224.6 34.2 %collective-permute-start.7 = (f32[16,48,896]{2,1,0:T(8,128)}, f32[16,48,896]{2,1,0:T(8,128)}, u32[]{:S(2)}, u32[]{:S(2)}) collective-permute-start(f32[16,48,896]{2,1,0:T(8,128)} %get-tuple-element.94), channel_id=1, source_target_pairs={{0,8},{1,9},{2,10},{3,11},{4,12},{5,13},{6,14},{7,15},{8,0},{9,1},... | collective-permute-start | bytes 8257544 | tf_op jit(solution)/shard_map/ppermute | solution.py:491
  238.1 73.3 %collective-permute-start.14 = (f32[16,48,1536]{2,1,0:T(8,128)}, f32[16,48,1536]{2,1,0:T(8,128)S(1)}, u32[]{:S(2)}, u32[]{:S(2)}) collective-permute-start(f32[16,48,1536]{2,1,0:T(8,128)} %get-tuple-element.99), channel_id=1, source_target_pairs={{0,8},{1,9},{2,10},{3,11},{4,12},{5,13},{6,14},{7,15},{8,0},{9,1},... | collective-permute-start | bytes 14155784 | tf_op jit(solution)/shard_map/ppermute | solution.py:491
  240.1 16.3 %collective-permute-start.1 = (f32[8,48,768]{2,1,0:T(8,128)S(1)}, f32[8,48,768]{2,1,0:T(8,128)S(1)}, u32[]{:S(2)}, u32[]{:S(2)}) collective-permute-start(f32[8,48,768]{2,1,0:T(8,128)S(1)} %slice_add_fusion.7), channel_id=1, source_target_pairs={{0,1},{1,0},{2,3},{3,2},{4,5},{5,4},{6,7},{7,6},{8,10},{9,11},{10,... | collective-permute-start | bytes 3538952 | tf_op jit(solution)/shard_map/ppermute | solution.py:491
  258.0 9.9 %collective-permute-start.2 = (f32[4,48,768]{2,1,0:T(8,128)S(1)}, f32[4,48,768]{2,1,0:T(8,128)S(1)}, u32[]{:S(2)}, u32[]{:S(2)}) collective-permute-start(f32[4,48,768]{2,1,0:T(8,128)S(1)} %get-tuple-element.159), channel_id=1, source_target_pairs={{0,2},{1,3},{2,0},{3,1},{4,6},{5,7},{6,4},{7,5},{8,24},{9,25},{10,... | collective-permute-start | bytes 1769480 | tf_op jit(solution)/shard_map/ppermute | solution.py:491
  261.5 44.3 %collective-permute-start.8 = (f32[8,48,896]{2,1,0:T(8,128)}, f32[8,48,896]{2,1,0:T(8,128)S(1)}, u32[]{:S(2)}, u32[]{:S(2)}) collective-permute-start(f32[8,48,896]{2,1,0:T(8,128)} %slice_add_fusion.2), channel_id=1, source_target_pairs={{0,16},{1,17},{2,18},{3,19},{4,20},{5,21},{6,22},{7,23},{8,9},{9,8... | collective-permute-start | bytes 4128776 | tf_op jit(solution)/shard_map/ppermute | solution.py:491
  268.0 16.0 %collective-permute-start.3 = (f32[2,48,768]{2,1,0:T(8,128)S(1)}, f32[2,48,768]{2,1,0:T(8,128)S(1)}, u32[]{:S(2)}, u32[]{:S(2)}) collective-permute-start(f32[2,48,768]{2,1,0:T(8,128)S(1)} %get-tuple-element.173), channel_id=1, source_target_pairs={{0,16},{1,17},{2,18},{3,19},{4,20},{5,21},{6,22},{7,23},{8,9},{9,8... | collective-permute-start | bytes 884744 | tf_op jit(solution)/shard_map/ppermute | solution.py:491
  284.8 13.0 %collective-permute-start.4 = (f32[1,48,768]{2,1,0:T(8,128)}, f32[1,48,768]{2,1,0:T(8,128)}, u32[]{:S(2)}, u32[]{:S(2)}) collective-permute-start(f32[1,48,768]{2,1,0:T(8,128)} %slice_add_fusion.26), channel_id=1, source_target_pairs={{0,4},{1,5},{2,6},{3,7},{4,0},{5,1},{6,2},{7,3},{8,12},{9,13},{10,... | collective-permute-start | bytes 442376 | tf_op jit(solution)/shard_map/ppermute | solution.py:491
  299.6 61.5 %collective-permute-start.5 = (f32[1,48,768]{2,1,0:T(8,128)}, f32[1,48,768]{2,1,0:T(8,128)}, u32[]{:S(2)}, u32[]{:S(2)}) collective-permute-start(f32[1,48,768]{2,1,0:T(8,128)} %fusion.12), channel_id=1, source_target_pairs={{0,16},{1,17},{2,18},{3,19},{4,20},{5,21},{6,22},{7,23},{8,24},{9,... | collective-permute-start | bytes 442376 | tf_op jit(solution)/shard_map/ppermute | solution.py:491
  305.3 75.6 %collective-permute-start.22 = (f32[8,192,384]{2,1,0:T(8,128)}, f32[8,192,384]{2,1,0:T(8,128)}, u32[]{:S(2)}, u32[]{:S(2)}) collective-permute-start(f32[8,192,384]{2,1,0:T(8,128)} %slice_add_fusion), channel_id=1, source_target_pairs={{0,16},{1,17},{2,18},{3,19},{4,20},{5,21},{6,22},{7,23},{8,9},{9,8... | collective-permute-start | bytes 7077896 | tf_op jit(solution)/shard_map/ppermute | solution.py:491
  309.9 52.4 %collective-permute-start.9 = (f32[4,48,896]{2,1,0:T(8,128)}, f32[4,48,896]{2,1,0:T(8,128)S(1)}, u32[]{:S(2)}, u32[]{:S(2)}) collective-permute-start(f32[4,48,896]{2,1,0:T(8,128)} %get-tuple-element.157), channel_id=1, source_target_pairs={{0,1},{1,0},{2,3},{3,2},{4,5},{5,4},{6,7},{7,6},{8,10},{9,11},{10,... | collective-permute-start | bytes 2064392 | tf_op jit(solution)/shard_map/ppermute | solution.py:491
  314.2 70.1 %collective-permute-start.15 = (f32[8,48,1536]{2,1,0:T(8,128)}, f32[8,48,1536]{2,1,0:T(8,128)}, u32[]{:S(2)}, u32[]{:S(2)}) collective-permute-start(f32[8,48,1536]{2,1,0:T(8,128)} %slice_add_fusion.1), channel_id=1, source_target_pairs={{0,2},{1,3},{2,0},{3,1},{4,6},{5,7},{6,4},{7,5},{8,24},{9,25},{10,... | collective-permute-start | bytes 7077896 | tf_op jit(solution)/shard_map/ppermute | solution.py:491
  316.6 44.4 %all-to-all-start.4 = ((f32[32,1,384]{2,1,0:T(1,128)}), f32[32,1,384]{2,1,0:T(1,128)S(1)}, u32[]{:S(2)}, u32[]{:S(2)}) async-start(f32[32,1,384]{2,1,0:T(1,128)} %all_to_all.22), calls=%async_computation.4 | async-start | bytes 98304 | tf_op jit(solution)/shard_map/all_to_all | solution.py:569
  362.1 2.4 collective-permute-start.6
  362.4 7.3 %collective-permute-start.10 = (f32[2,48,896]{2,1,0:T(8,128)S(1)}, f32[2,48,896]{2,1,0:T(8,128)S(1)}, u32[]{:S(2)}, u32[]{:S(2)}) collective-permute-start(f32[2,48,896]{2,1,0:T(8,128)S(1)} %get-tuple-element.167), channel_id=1, source_target_pairs={{0,2},{1,3},{2,0},{3,1},{4,6},{5,7},{6,4},{7,5},{8,24},{9,25},{10,... | collective-permute-start | bytes 1032200 | tf_op jit(solution)/shard_map/ppermute | solution.py:491
  369.7 10.5 %collective-permute-start.11 = (f32[1,48,896]{2,1,0:T(8,128)S(1)}, f32[1,48,896]{2,1,0:T(8,128)S(1)}, u32[]{:S(2)}, u32[]{:S(2)}) collective-permute-start(f32[1,48,896]{2,1,0:T(8,128)S(1)} %slice_add_fusion.24), channel_id=1, source_target_pairs={{0,4},{1,5},{2,6},{3,7},{4,0},{5,1},{6,2},{7,3},{8,12},{9,13},{10,... | collective-permute-start | bytes 516104 | tf_op jit(solution)/shard_map/ppermute | solution.py:491
  380.2 9.0 %collective-permute-start.12 = (f32[1,48,896]{2,1,0:T(8,128)S(1)}, f32[1,48,896]{2,1,0:T(8,128)S(1)}, u32[]{:S(2)}, u32[]{:S(2)}) collective-permute-start(f32[1,48,896]{2,1,0:T(8,128)S(1)} %fusion.11), channel_id=1, source_target_pairs={{0,16},{1,17},{2,18},{3,19},{4,20},{5,21},{6,22},{7,23},{8,24},{9,... | collective-permute-start | bytes 516104 | tf_op jit(solution)/shard_map/ppermute | solution.py:491
  383.7 27.1 %collective-permute-start.23 = (f32[4,192,384]{2,1,0:T(8,128)S(1)}, f32[4,192,384]{2,1,0:T(8,128)S(1)}, u32[]{:S(2)}, u32[]{:S(2)}) collective-permute-start(f32[4,192,384]{2,1,0:T(8,128)S(1)} %get-tuple-element.153), channel_id=1, source_target_pairs={{0,1},{1,0},{2,3},{3,2},{4,5},{5,4},{6,7},{7,6},{8,10},{9,11},{10,... | collective-permute-start | bytes 3538952 | tf_op jit(solution)/shard_map/ppermute | solution.py:491
  387.7 23.3 %collective-permute-start.16 = (f32[4,48,1536]{2,1,0:T(8,128)S(1)}, f32[4,48,1536]{2,1,0:T(8,128)S(1)}, u32[]{:S(2)}, u32[]{:S(2)}) collective-permute-start(f32[4,48,1536]{2,1,0:T(8,128)S(1)} %get-tuple-element.155), channel_id=1, source_target_pairs={{0,16},{1,17},{2,18},{3,19},{4,20},{5,21},{6,22},{7,23},{8,9},{9,8... | collective-permute-start | bytes 3538952 | tf_op jit(solution)/shard_map/ppermute | solution.py:491
  389.3 1.7 collective-permute-start.13
  410.9 18.7 %collective-permute-start.24 = (f32[2,192,384]{2,1,0:T(8,128)S(1)}, f32[2,192,384]{2,1,0:T(8,128)S(1)}, u32[]{:S(2)}, u32[]{:S(2)}) collective-permute-start(f32[2,192,384]{2,1,0:T(8,128)S(1)} %get-tuple-element.161), channel_id=1, source_target_pairs={{0,2},{1,3},{2,0},{3,1},{4,6},{5,7},{6,4},{7,5},{8,24},{9,25},{10,... | collective-permute-start | bytes 1769480 | tf_op jit(solution)/shard_map/ppermute | solution.py:491
  411.1 18.6 %collective-permute-start.17 = (f32[2,48,1536]{2,1,0:T(8,128)S(1)}, f32[2,48,1536]{2,1,0:T(8,128)S(1)}, u32[]{:S(2)}, u32[]{:S(2)}) collective-permute-start(f32[2,48,1536]{2,1,0:T(8,128)S(1)} %get-tuple-element.163), channel_id=1, source_target_pairs={{0,1},{1,0},{2,3},{3,2},{4,5},{5,4},{6,7},{7,6},{8,10},{9,11},{10,... | collective-permute-start | bytes 1769480 | tf_op jit(solution)/shard_map/ppermute | solution.py:491
  429.6 19.3 %collective-permute-start.25 = (f32[1,192,384]{2,1,0:T(8,128)S(1)}, f32[1,192,384]{2,1,0:T(8,128)}, u32[]{:S(2)}, u32[]{:S(2)}) collective-permute-start(f32[1,192,384]{2,1,0:T(8,128)S(1)} %slice_add_fusion.18), channel_id=1, source_target_pairs={{0,4},{1,5},{2,6},{3,7},{4,0},{5,1},{6,2},{7,3},{8,12},{9,13},{10,... | collective-permute-start | bytes 884744 | tf_op jit(solution)/shard_map/ppermute | solution.py:491
  429.8 22.3 %collective-permute-start.18 = (f32[1,48,1536]{2,1,0:T(8,128)S(1)}, f32[1,48,1536]{2,1,0:T(8,128)}, u32[]{:S(2)}, u32[]{:S(2)}) collective-permute-start(f32[1,48,1536]{2,1,0:T(8,128)S(1)} %slice_add_fusion.20), channel_id=1, source_target_pairs={{0,4},{1,5},{2,6},{3,7},{4,0},{5,1},{6,2},{7,3},{8,12},{9,13},{10,... | collective-permute-start | bytes 884744 | tf_op jit(solution)/shard_map/ppermute | solution.py:491
  449.9 9.1 %collective-permute-start.26 = (f32[1,192,384]{2,1,0:T(8,128)S(1)}, f32[1,192,384]{2,1,0:T(8,128)S(1)}, u32[]{:S(2)}, u32[]{:S(2)}) collective-permute-start(f32[1,192,384]{2,1,0:T(8,128)S(1)} %fusion.9), channel_id=1, source_target_pairs={{0,16},{1,17},{2,18},{3,19},{4,20},{5,21},{6,22},{7,23},{8,24},{9,... | collective-permute-start | bytes 884744 | tf_op jit(solution)/shard_map/ppermute | solution.py:491
  453.1 9.1 %collective-permute-start.19 = (f32[1,48,1536]{2,1,0:T(8,128)S(1)}, f32[1,48,1536]{2,1,0:T(8,128)S(1)}, u32[]{:S(2)}, u32[]{:S(2)}) collective-permute-start(f32[1,48,1536]{2,1,0:T(8,128)S(1)} %fusion.10), channel_id=1, source_target_pairs={{0,16},{1,17},{2,18},{3,19},{4,20},{5,21},{6,22},{7,23},{8,24},{9,... | collective-permute-start | bytes 884744 | tf_op jit(solution)/shard_map/ppermute | solution.py:491
  459.3 3.7 collective-permute-start.27
  462.2 2.1 collective-permute-start.20
  (26 other events, 215.8 us)

commit v2 on v1

--- a/solution.py
+++ b/solution.py
@@ -49,12 +49,41 @@
     return scale * (scaled - jnp.mean(scaled, axis=1, keepdims=True) - unit * along)
 
 
+def last_start(starts_ref):
+    starts = starts_ref[...]
+    at = lax.broadcasted_iota(jnp.int32, starts.shape, 1)
+    return jnp.max(jnp.where(starts > 0, at, -1), axis=1, keepdims=True)
+
+
+def pack_carry(packed_ref, state_ref, norm_ref, last):
+    count, rows, lanes = packed_ref.shape
+    share = rows - 2
+    keep = jnp.broadcast_to(jnp.where(last < 0, 1.0, 0.0), (1, lanes))
+    for place in range(count):
+        packed_ref[place, :share, :] = state_ref[place * share : (place + 1) * share, :]
+        row = norm_ref[place : place + 1, :] if place < norm_ref.shape[0] else jnp.zeros((1, lanes), f32)
+        packed_ref[place, share : share + 1, :] = row
+        packed_ref[place, share + 1 :, :] = keep
+
+
+def unpack_carry(packed_ref, state_ref, norm_ref):
+    count, rows, _ = packed_ref.shape
+    share = rows - 2
+    for place in range(count):
+        state_ref[place * share : (place + 1) * share, :] = packed_ref[place, :share, :]
+    for place in range(norm_ref.shape[0]):
+        norm_ref[place : place + 1, :] = packed_ref[place, share : share + 1, :]
+
+
 def enter_kernel(
-    x_ref, gains_ref, w_ref, fq_ref, fk_ref, tail_ref,
-    hid_ref, qkv_ref, pq_ref, pk_ref, state_ref, norm_ref, logit_ref,
+    x_ref, gains_ref, w_ref, fq_ref, fk_ref, starts_ref,
+    hid_ref, qkv_ref, pq_ref, pk_ref, packed_ref, logit_ref, state_ref, norm_ref,
 ):
     head_dim, width = fq_ref.shape
     rows = x_ref.shape[0]
+    last = last_start(starts_ref)
+    at = lax.broadcasted_iota(jnp.int32, (1, rows), 1) + pl.program_id(0) * rows
+    tail = jnp.where(at >= last, 1.0, 0.0).astype(bf16)
     unit, _ = norm_parts(x_ref[...].astype(f32))
     hid = (unit * gains_ref[0:1, :] + gains_ref[1:2, :]).astype(bf16)
     hid_ref[...] = hid.T
@@ -90,9 +119,13 @@
     for head in range(heads):
         low, high = (head * head_dim, (head + 1) * head_dim)
         wide = stacked(qkv_ref[2 * width + low : 2 * width + high, :], ones)
-        local = dg(wide, pk_ref[2 * low : 2 * high, :] * tail_ref[...], 1, 1)
+        local = dg(wide, pk_ref[2 * low : 2 * high, :] * tail, 1, 1)
         state_ref[low:high, :] += local[:head_dim]
         norm_ref[head : head + 1, :] += local[head_dim : head_dim + 1]
+
+    @pl.when(pl.program_id(0) == pl.num_programs(0) - 1)
+    def _():
+        pack_carry(packed_ref, state_ref, norm_ref, last)
 
 
 def masked(scores, start, first, offset):
@@ -133,11 +166,11 @@
 
 
 def block_kernel(
-    num0_ref, num1_ref, den0_ref, den1_ref, pq_ref, state_ref, norm_ref, open_ref, x_ref, cot_ref, gains_ref,
+    num0_ref, num1_ref, den0_ref, den1_ref, pq_ref, home_ref, starts_ref, open_ref, x_ref, cot_ref, gains_ref,
     wout_ref, wfc_ref, wproj_ref,
     low_ref, hid_ref, act_ref, dpre_ref, out_ref, dbranch_ref, dresid_ref, dnum_ref, dden_ref,
-    gstate_ref, gnorm_ref, sums_ref,
-    mixed_ref, inverse_ref,
+    packed_ref, sums_ref, state_ref, norms_ref,
+    mixed_ref, inverse_ref, norm_ref, gstate_ref, gnorm_ref,
 ):
     width, features = state_ref.shape
     head_dim = features // 2
@@ -146,6 +179,9 @@
 
     @pl.when(pl.program_id(0) == 0)
     def _():
+        unpack_carry(home_ref, state_ref, norm_ref)
+        for head in range(norm_ref.shape[0]):
+            norms_ref[head] = norm_ref[head : head + 1, :]
         gstate_ref[...] = jnp.zeros_like(gstate_ref)
         gnorm_ref[...] = jnp.zeros_like(gnorm_ref)
         sums_ref[...] = jnp.zeros_like(sums_ref)
@@ -217,6 +253,10 @@
         gstate_ref[low:high, :] += local[:head_dim] + local[head_dim:features]
         gnorm_ref[head : head + 1, :] += local[features : features + 1] + local[features + 1 : features + 2]
 
+    @pl.when(pl.program_id(0) == pl.num_programs(0) - 1)
+    def _():
+        pack_carry(packed_ref, gstate_ref, gnorm_ref, last_start(starts_ref))
+
 
 def logit_back(phi, dphi):
     half = phi.shape[0] // 2
@@ -281,13 +321,20 @@
 
 
 def key_back_kernel(
-    pk_ref, k_ref, v_ref, dphik0_ref, dphik1_ref, dv0_ref, dv1_ref, tail_ref, state_ref, norm_ref, fk_ref,
-    dkv_ref, gfk_ref,
+    pk_ref, k_ref, v_ref, dphik0_ref, dphik1_ref, dv0_ref, dv1_ref, tail_ref, home_ref, fk_ref,
+    dkv_ref, gfk_ref, state_ref, norm_ref,
 ):
     features, tokens = pk_ref.shape
     head_dim = features // 2
-    state_high, state_low = parts_of(state_ref[...])
-    carried = stacked(state_high, state_low, rows_of(parts_of(norm_ref[0]), features))
+    head = pl.program_id(0)
+
+    @pl.when(head == 0)
+    def _():
+        unpack_carry(home_ref, state_ref, norm_ref)
+
+    first = pl.multiple_of(head * head_dim, head_dim)
+    state_high, state_low = parts_of(state_ref[pl.ds(first, head_dim), :])
+    carried = stacked(state_high, state_low, rows_of(parts_of(norm_ref[pl.ds(head, 1), :]), features))
     values = v_ref[...]
     tail = tail_ref[...]
     wide = stacked(values, values, jnp.ones((16, tokens), bf16))
@@ -414,7 +461,22 @@
     return jnp.concatenate([theirs ^ theirs[own], mine ^ mine[own], core[None].astype(jnp.int32)])
 
 
-def product_kernel(counts, theirs, mine, by_columns, table_ref, *refs):
+def product_kernel(counts, theirs, mine, last_forms, by_columns, table_ref, *refs):
+    if last_forms is None:
+        product_step(counts, theirs, mine, by_columns, table_ref, refs)
+        return
+    last = pl.num_programs(0) - 1
+
+    @pl.when(pl.program_id(0) < last)
+    def _():
+        product_step(counts, theirs, mine, by_columns, table_ref, refs)
+
+    @pl.when(pl.program_id(0) == last)
+    def _():
+        product_step(counts, *last_forms, by_columns, table_ref, refs)
+
+
+def product_step(counts, theirs, mine, by_columns, table_ref, refs):
     count, tails = counts
     ins, refs = (refs[:count], refs[count:])
     tail_refs, refs = (refs[:tails], refs[tails:])
@@ -461,7 +523,7 @@
                 give_ref[slot - half, :, span] = part
 
 
-def products(table, theirs, mine, ins, specs, grid, piece, tail=None, by_columns=False):
+def products(table, theirs, mine, ins, specs, grid, piece, tail=None, by_columns=False, last=None):
     pieces = (table.shape[0] - 1) // 2
     if by_columns or grid == 1:
         block = lambda count: pl.BlockSpec((count,) + piece, lambda i, t: (0, 0, 0))
@@ -476,7 +538,7 @@
         specs.append(pl.BlockSpec((1,) + tail.shape[1:], lambda i, t: (t[2 * pieces], 0, 0)))
     counts = (pieces, pieces // 2, pieces // 2)
     return pl.pallas_call(
-        partial(product_kernel, (count, len(ins) - count), theirs, mine, by_columns),
+        partial(product_kernel, (count, len(ins) - count), theirs, mine, last, by_columns),
         grid_spec=pltpu.PrefetchScalarGridSpec(
             num_scalar_prefetch=1, grid=(grid,), in_specs=specs, out_specs=[block(c) for c in counts]
         ),
@@ -532,30 +594,19 @@
         block = count - 1 - at if backward else at
         out_ref[block] = so_far
         local = got_ref[block]
-        return local + local[rows - 1 :, lanes - 1 :] * so_far
+        return local + local[rows - 1 :, :] * so_far
 
     lax.fori_loop(0, count, step, jnp.zeros((rows, lanes), f32), unroll=8)
 
 
-def carry_scan(state, norm, keep, backward):
-    grp_size, tok_size = sizes()
-    count = grp_size * tok_size
-    lanes = state.shape[1]
-    share = state.shape[0] // count
-    spare = norm.size // count
-    extra = jnp.concatenate(
-        [norm.reshape(count, spare), jnp.zeros((count, lanes - 1 - spare), f32), jnp.full((count, 1), keep)],
-        axis=1,
-    )
-    packed = jnp.concatenate([state.reshape(count, share, lanes), extra[:, None]], axis=1)
+def carry_scan(packed, backward):
     landed = lax.all_to_all(packed, ("grp", "tok"), 0, 0, tiled=True)
     summed = pl.pallas_call(
         partial(chain_kernel, backward),
         out_shape=shape_of(landed.shape, f32),
         compiler_params=pltpu.CompilerParams(vmem_limit_bytes=grant),
     )(landed)
-    home = lax.all_to_all(summed, ("grp", "tok"), 0, 0, tiled=True)
-    return home[:, :share].reshape(state.shape), home[:, share, :spare].reshape(norm.shape)
+    return lax.all_to_all(summed, ("grp", "tok"), 0, 0, tiled=True)
 
 
 def reduce_vectors(stack):
@@ -600,21 +651,25 @@
     start = jnp.maximum(last, 0)[None]
     opened = (last < 0).astype(f32)[None]
     tail = (at >= last[-1]).astype(f32)[None]
-    keep = (last[-1] < 0).astype(f32)
-
-    hid1, qkv, phi_q, phi_k, state, norm = call(
+    starts = doc_starts[None]
+    grp_size, tok_size = sizes()
+    count = grp_size * tok_size
+    carry_shape = (count, width // count + 2, feats)
+    carry_block = pl.BlockSpec(carry_shape, lambda i: (0, 0, 0))
+
+    hid1, qkv, phi_q, phi_k, packed = call(
         enter_kernel, blocks,
         [down(rows, width), whole((4, width)), whole(w_qkv.shape),
-         whole((head_dim, width)), whole((head_dim, width)), across(1, rows)],
+         whole((head_dim, width)), whole((head_dim, width)), whole((1, tokens))],
         [across(width, rows), across(3 * width, rows), across(2 * width, rows), across(2 * width, rows),
-         whole((width, feats)), whole((heads, feats))],
+         carry_block],
         [shape_of((width, tokens), bf16), shape_of((3 * width, tokens), bf16),
          shape_of((2 * width, tokens), bf16), shape_of((2 * width, tokens), bf16),
-         shape_of((width, feats), f32), shape_of((heads, feats), f32)],
-        (layer_input, gains, w_qkv, feat_q.T, feat_k.T, tail.astype(bf16)),
-        [pltpu.VMEM((2 * width, rows), f32)],
-    )
-    state_in, norm_in = carry_scan(state, norm, keep, False)
+         shape_of(carry_shape, f32)],
+        (layer_input, gains, w_qkv, feat_q.T, feat_k.T, starts),
+        [pltpu.VMEM((2 * width, rows), f32), pltpu.VMEM((width, feats), f32), pltpu.VMEM((heads, feats), f32)],
+    )
+    home = carry_scan(packed, False)
     part = heads // 2
     locals_ = [
         call(
@@ -628,34 +683,39 @@
         for at in range(2)
     ]
     once = lambda shape: pl.BlockSpec(shape, lambda i: (0, 0), pipeline_mode=pl.Buffered(1))
-    mixed_low, hid2, act, dpre, output, dbranch, dresid, dnum, dden, back_state, back_norm, sums2 = call(
+    mixed_low, hid2, act, dpre, output, dbranch, dresid, dnum, dden, back_packed, sums2, state_in, norms_in = call(
         block_kernel, blocks,
         [across(width // 2, rows), across(width // 2, rows), heads_across(part, rows),
-         heads_across(part, rows), across(2 * width, rows), whole((width, feats)),
-         whole((heads, feats)), across(1, rows), down(rows, width), down(rows, width), whole((4, width)),
+         heads_across(part, rows), across(2 * width, rows), carry_block,
+         whole((1, tokens)), across(1, rows), down(rows, width), down(rows, width), whole((4, width)),
          once(w_out.shape), once(w_fc.shape), once(w_proj.shape)],
         [across(width, rows), across(width, rows), down(rows, hidden), down(rows, hidden),
          down(rows, width), down(rows, width), down(rows, width), across(width, rows),
-         heads_across(heads, rows), whole((width, feats)), whole((heads, feats)), whole((8, width))],
+         heads_across(heads, rows), carry_block, whole((8, width)), whole((width, feats)),
+         whole((heads, 1, feats))],
         [shape_of((width, tokens), bf16), shape_of((width, tokens), bf16), shape_of((tokens, hidden), bf16),
          shape_of((tokens, hidden), bf16), shape_of((tokens, width), bf16), shape_of((tokens, width), bf16),
          shape_of((tokens, width), f32), shape_of((width, tokens), f32), shape_of((heads, 1, tokens), f32),
-         shape_of((width, feats), f32), shape_of((heads, feats), f32), shape_of((8, width), f32)],
-        (locals_[0][0], locals_[1][0], locals_[0][1], locals_[1][1], phi_q, state_in, norm_in, opened,
+         shape_of(carry_shape, f32), shape_of((8, width), f32), shape_of((width, feats), f32),
+         shape_of((heads, 1, feats), f32)],
+        (locals_[0][0], locals_[1][0], locals_[0][1], locals_[1][1], phi_q, home, starts, opened,
          layer_input, cotangent, gains, w_out, w_fc, w_proj),
-        [pltpu.VMEM((width, rows), f32), pltpu.VMEM((16, rows), f32)],
+        [pltpu.VMEM((width, rows), f32), pltpu.VMEM((16, rows), f32), pltpu.VMEM((heads, feats), f32),
+         pltpu.VMEM((width, feats), f32), pltpu.VMEM((heads, feats), f32)],
     )
     half = width // 2
     fars, toks = (lax.axis_size("grp") // 2, lax.axis_size("tok"))
     piece_rows = width // (fars * toks)
-    turns_a, turns_b, turns_c, turns_d = ((0, 1), (2, 0), (1, 2), (0, 1))
+    turns_a, turns_b, turns_c, turns_d = ((0, 1), (2, 0), (2, 0), (0, 1))
     table_a, table_b, table_c, table_d = map(tables_of, (turns_a, turns_b, turns_c, turns_d))
     last_at = table_a.shape[0] - 1
     plain = lambda rows_: pl.BlockSpec((rows_, tokens), lambda i, t: (0, 0))
     which = lambda turn, t: t[last_at] if turn else 1 - t[last_at]
     right_half = lambda turn: pl.BlockSpec((tokens, half), lambda i, t: (0, which(turn, t)))
     chosen = lambda row, turn: pl.BlockSpec((1, half, tokens), lambda i, t: (row, which(turn, t), 0))
-    quarter = lambda turn: pl.BlockSpec((tokens, hidden // 8), lambda i, t: (0, 4 * which(turn, t) + i))
+    quarter = lambda turn: pl.BlockSpec(
+        (tokens, half), lambda i, t: (0, hidden // width * which(turn, t) + jnp.minimum(i, hidden // width - 1))
+    )
     theirs_a, keep_a, give_a = products(
         table_a, ((0, 2, 0, 0),), ((1, 2, 0, 0),), (cotangent, cotangent, act),
         (right_half(0), right_half(1), pl.BlockSpec((tokens, hidden // 4), lambda i, t: (0, i))),
@@ -663,11 +723,14 @@
     )
     other_a = swap_cores(theirs_a)
     theirs_b, keep_b, give_b = products(
-        table_b, ((0, 1, 1, 0),), ((0, 2, 1, 0),), (hid2, dpre, dpre),
-        (plain(width), quarter(0), quarter(1)), 4, (piece_rows, hidden // 2),
+        table_b, ((0, 1, 1, 0),), ((0, 2, 1, 0),),
+        (hid2, dpre, dpre, mixed_low, dbranch, dbranch),
+        (plain(width), quarter(0), quarter(1), plain(width), right_half(0), right_half(1)),
+        hidden // width + 1, (piece_rows, hidden // 2 + half),
+        last=(((3, 4, 1, 0),), ((3, 5, 1, 0),)),
     )
     other_b = swap_cores(theirs_b)
-    state_back, norm_back_in = carry_scan(back_state, back_norm, keep, True)
+    returned = carry_scan(back_packed, True)
     split = [
         call(
             local_back_kernel, part,
@@ -680,7 +743,7 @@
              head_rows(feats, tokens), head_rows(head_dim, tokens)],
             [shape_of((width // 2, tokens), bf16), shape_of((part, head_dim, head_dim), f32),
              shape_of((width, tokens), f32), shape_of((width // 2, tokens), f32)],
-            (phi_q, phi_k, qkv, qkv, dnum, dden, start, opened, state_in, norm_in[:, None], feat_q),
+            (phi_q, phi_k, qkv, qkv, dnum, dden, start, opened, state_in, norms_in, feat_q),
         )
         for at in range(2)
     ]
@@ -691,11 +754,12 @@
         key_back_kernel, heads,
         [head_rows(feats, tokens), head_rows(head_dim, tokens, heads),
          head_rows(head_dim, tokens, 2 * heads), lower(feats), upper(feats), lower(head_dim), upper(head_dim),
-         whole((1, tokens)), head_rows(head_dim, feats), one_head(feats), head_rows(head_dim, head_dim)],
+         whole((1, tokens)), carry_block, head_rows(head_dim, head_dim)],
         [pl.BlockSpec((2, head_dim, tokens), lambda i: (0, i, 0)),
          pl.BlockSpec((1, head_dim, head_dim), lambda i: (i, 0, 0))],
         [shape_of((2, width, tokens), bf16), shape_of((heads, head_dim, head_dim), f32)],
-        (phi_k, qkv, qkv, split[0][2], split[1][2], split[0][3], split[1][3], tail, state_back, norm_back_in[:, None], feat_k),
+        (phi_k, qkv, qkv, split[0][2], split[1][2], split[0][3], split[1][3], tail, returned, feat_k),
+        [pltpu.VMEM((width, feats), f32), pltpu.VMEM((heads, feats), f32)],
     )
     grad_input, sums1 = call(
         leave_kernel, blocks,
@@ -711,10 +775,8 @@
     theirs_q = jnp.where(first_core, split[1][0], split[0][0])
     mine_q = jnp.where(first_core, split[0][0], split[1][0])
     theirs_c, keep_c, give_c = products(
-        table_c, ((0, 1, 1, 0), (3, 4, 1, 1)), ((0, 2, 1, 0), (3, 5, 1, 1)),
-        (mixed_low, dbranch, dbranch, hid1, theirs_q, mine_q),
-        (plain(width), right_half(0), right_half(1), plain(width), plain(half), plain(half)),
-        1, (piece_rows, 2 * half),
+        table_c, ((0, 1, 1, 1),), ((0, 2, 1, 1),), (hid1, theirs_q, mine_q),
+        (plain(width), plain(half), plain(half)), 1, (piece_rows, half),
     )
     other_c = swap_cores(theirs_c)
     feats_both = jnp.stack([gfq.reshape(width, head_dim), gfk.reshape(width, head_dim)])
@@ -728,13 +790,16 @@
     )
     other_d = swap_cores(theirs_d)
     vectors = reduce_vectors(jnp.concatenate([sums1[:2], sums2[:2]], axis=0))
-    grad_proj = jnp.concatenate(fold(keep_a, give_a, other_a, turns_a), axis=0).T
-    grad_fc = jnp.concatenate(fold(keep_b, give_b, other_b, turns_b), axis=1)
+    a_pair = fold(keep_a, give_a, other_a, turns_a)
+    b_pair = fold(keep_b, give_b, other_b, turns_b)
     c_pair = fold(keep_c, give_c, other_c, turns_c)
     d_pair = fold(keep_d, give_d, other_d, turns_d)
-    grad_out = jnp.concatenate([part[:, :half] for part in c_pair], axis=1)
+    inner = hidden // 2
+    grad_proj = jnp.concatenate(a_pair, axis=0).T
+    grad_fc = jnp.concatenate([part[:, :inner] for part in b_pair], axis=1)
+    grad_out = jnp.concatenate([part[:, inner:] for part in b_pair], axis=1)
     grad_qkv = jnp.concatenate(
-        [part[:, half:] for part in c_pair]
+        list(c_pair)
         + [part[:, :half] for part in d_pair]
         + [part[:, half : 2 * half] for part in d_pair],
         axis=1,

time: 468 us -> 446 us (0.953)
  blocking collectives: 23.5 us -> 0 us
  starting transfers between devices: 36.5 us -> 47.1 us
    all_to_all x1, waiting for transfers between devices: 41.8 us -> 7.22 us  [reduce_vectors(): landed = lax.all_to_all(spread, ('grp', 'tok'), 0, 0, tiled=True)]
    all_to_all x1 -> x0, blocking collectives: 23.5 us -> none  [carry_scan(): landed = lax.all_to_all(packed, ('grp', 'tok'), 0, 0, tiled=True)]
    ppermute x28, waiting for transfers between devices: 111 us -> 130 us  [send(): return lax.ppermute(value, ('grp', 'tok'), flips(first, second))]
    all_to_all x1 -> x2, waiting for transfers between devices: 5.17 us -> 18.8 us  [carry_scan(): landed = lax.all_to_all(packed, ('grp', 'tok'), 0, 0, tiled=True)]
    all_to_all x1 -> x2, starting transfers between devices: 5.66 us -> 13.4 us  [carry_scan(): landed = lax.all_to_all(packed, ('grp', 'tok'), 0, 0, tiled=True)]
    add x8, other arithmetic: 10.1 us -> 14.8 us  [fold(): keep = keep[:half] + landed_of(0, half)]
  transfers between devices with their start and end apart: 32 -> 33, of which waited for: 16 -> 15; matrix products, arithmetic and copies ran while one was open for 11% -> 12% of each run, Pallas kernels for 19% -> 23%
where the time goes in v2:
time: 446 us; the launch traced here: 444 us
  Pallas kernels  176 us (39%)
  waiting for transfers between devices  156 us (35%)
  starting transfers between devices  47.1 us (11%)
  other arithmetic  44.8 us (10%)
  local copies, waits for them, and re-layouts  18.7 us (4%)
    ppermute x28, waiting for transfers between devices, send(): return lax.ppermute(value, ('grp', 'tok'), flips(first, second))  130 us
    pallas_call x8, Pallas kernels, call(): pl.pallas_call(kernel, grid=(grid,), in_specs=ins, out_specs=outs, out_sh...  128 us
    pallas_call x4, Pallas kernels, products(): pl.pallas_call(partial(product_kernel, (count, len(ins) - count), theirs,...  44.1 us
    ppermute x28, starting transfers between devices, send(): return lax.ppermute(value, ('grp', 'tok'), flips(first, second))  23.5 us
    all_to_all x2, waiting for transfers between devices, carry_scan(): landed = lax.all_to_all(packed, ('grp', 'tok'), 0, 0, tiled=True)  18.8 us
    add x8, other arithmetic, fold(): keep = keep[:half] + landed_of(0, half)  14.8 us
    all_to_all x2, starting transfers between devices, carry_scan(): landed = lax.all_to_all(packed, ('grp', 'tok'), 0, 0, tiled=True)  13.4 us
    add x4, other arithmetic, fold(): give = give + other[count:]  9.71 us
  transfers between devices with their start and end apart: 33, of which 15 were waited for; matrix products, arithmetic and copies ran while one was open for 12% of the time, Pallas kernels for 23%

profile of v2, /device:TPU:0, one launch (start us, length us, event | category | flops | bytes accessed | tf_op | source)
XLA Modules:
  0.0 444.0 jit_solution(401303527308002968)
XLA Ops:
  4.0 15.7 %shard_map.292 = (bf16[768,1024]{1,0:T(8,128)(2,1)}, bf16[2304,1024]{1,0:T(8,128)(2,1)}, bf16[1536,1024]{1,0:T(8,128)(2,1)}, bf16[1536,1024]{1,0:T(8,128)(2,1)}, f32[32,26,128]{2,1,0:T(8,128)}) custom-call(bf16[1024,768]{1,0:T(8,128)(2,1)} %x_ref.5, f32[4,768]{1,0:T(4,128)} %pad_maximum_fusion.7.gains_ref, bf16[768,2304]{1,0:T(8,128)(2,1)} %w_ref.3, ...), custom_call_target="tpu_custom_call" | custom-call | tf_op jit(solution)/shard_map/pallas_call | solution.py:398
  19.7 7.4 %all-to-all-start = ((f32[32,26,128]{2,1,0:T(8,128)}), f32[32,26,128]{2,1,0:T(8,128)S(1)}, u32[]{:S(2)}, u32[]{:S(2)}) async-start(f32[32,26,128]{2,1,0:T(8,128)} %get-tuple-element.65), calls=%async_computation | async-start | bytes 1048576 | tf_op jit(solution)/shard_map/all_to_all | solution.py:603
  27.5 15.8 %all-to-all-done.got_ref = f32[32,26,128]{2,1,0:T(8,128)S(1)} async-done(((f32[32,26,128]{2,1,0:T(8,128)}), f32[32,26,128]{2,1,0:T(8,128)S(1)}, u32[]{:S(2)}, u32[]{:S(2)}) %all-to-all-start) | async-done | bytes 426016 | tf_op jit(solution)/shard_map/all_to_all | solution.py:603
  46.0 2.8 all-to-all-start.1
  49.4 7.6 %shard_map.294 = (f32[384,1024]{1,0:T(8,128)}, f32[6,1,1024]{2,1,0:T(1,128)}) custom-call(bf16[1536,1024]{1,0:T(8,128)(2,1)} %get-tuple-element.58.pq_ref, bf16[1536,1024]{1,0:T(8,128)(2,1)} %get-tuple-element.59.pk_ref, bf16[2304,1024]{1,0:T(8,128)(2,1)} %get-tuple-element.60.v_ref.q_ref.k_ref, s32[1,1024]{1,0:T(1,128)} %bitcast.32), custom_call_target="tpu_custom_call" | custom-call | tf_op jit(solution)/shard_map/pallas_call | solution.py:398
  57.1 7.7 %shard_map.293 = (f32[384,1024]{1,0:T(8,128)}, f32[6,1,1024]{2,1,0:T(1,128)}) custom-call(bf16[1536,1024]{1,0:T(8,128)(2,1)} %get-tuple-element.58.pq_ref, bf16[1536,1024]{1,0:T(8,128)(2,1)} %get-tuple-element.59.pk_ref, bf16[2304,1024]{1,0:T(8,128)(2,1)} %get-tuple-element.60.v_ref.q_ref.k_ref, s32[1,1024]{1,0:T(1,128)} %bitcast.33), custom_call_target="tpu_custom_call" | custom-call | tf_op jit(solution)/shard_map/pallas_call | solution.py:398
  71.7 39.8 %shard_map.296 = (bf16[768,1024]{1,0:T(8,128)(2,1)}, bf16[768,1024]{1,0:T(8,128)(2,1)}, bf16[1024,3072]{1,0:T(8,128)(2,1)}, bf16[1024,3072]{1,0:T(8,128)(2,1)}, ...) custom-call(f32[384,1024]{1,0:T(8,128)} %get-tuple-element.61.num0_r, ...), custom_call_target="tpu_custom_call" | custom-call | tf_op jit(solution)/shard_map/pallas_call | solution.py:398
  111.5 15.6 %shard_map.304 = (f32[16,48,1920]{2,1,0:T(8,128)}, f32[8,48,1920]{2,1,0:T(8,128)}, f32[8,48,1920]{2,1,0:T(8,128)}) custom-call(s32[33]{0:T(128)} %add_add_fusion.table_ref, bf16[768,1024]{1,0:T(8,128)(2,1)} %get-tuple-element.93.refs_0_, bf16[1024,3072]{1,0:T(8,128)(2,1)} %get-tuple-element.94.refs_1_.refs_2_, ...), custom_call_target="tpu_custom_call" | custom-call | tf_op jit(solution)/shard_map/pallas_call | solution.py:540
  127.0 6.0 %all-to-all-start.2 = ((f32[32,26,128]{2,1,0:T(8,128)}), f32[32,26,128]{2,1,0:T(8,128)S(1)}, u32[]{:S(2)}, u32[]{:S(2)}) async-start(f32[32,26,128]{2,1,0:T(8,128)} %get-tuple-element.77), calls=%async_computation.2 | async-start | bytes 1048576 | tf_op jit(solution)/shard_map/all_to_all | solution.py:603
  133.7 12.4 %shard_map.305 = (f32[16,192,384]{2,1,0:T(8,128)}, f32[8,192,384]{2,1,0:T(8,128)}, f32[8,192,384]{2,1,0:T(8,128)}) custom-call(s32[33]{0:T(128)} %add_add_fusion.1.table_ref, bf16[1024,768]{1,0:T(8,128)(2,1)} %refs_1_.1, bf16[1024,768]{1,0:T(8,128)(2,1)} %refs_1_.1, bf16[1024,3072]{1,0:T(8,128)(2,1)} %get-tuple-element.100.refs_2_), custom_call_target="tpu_custom_call" | custom-call | tf_op jit(solution)/shard_map/pallas_call | solution.py:540
  146.1 3.0 all-to-all-done.2.got_ref
  158.0 16.6 %shard_map.298 = (bf16[384,1024]{1,0:T(8,128)(2,1)}, f32[6,64,64]{2,1,0:T(8,128)}, f32[768,1024]{1,0:T(8,128)}, f32[384,1024]{1,0:T(8,128)}) custom-call(bf16[1536,1024]{1,0:T(8,128)(2,1)} %get-tuple-element.58.pq_ref, bf16[1536,1024]{1,0:T(8,128)(2,1)} %get-tuple-element.59.pk_ref, bf16[2304,1024]{1,0:T(8,128)(2,1)} %get-tuple-element.60.v_ref.q_ref.k_ref, ...), custom_call_target="tpu_custom_call" | custom-call | tf_op jit(solution)/shard_map/pallas_call | solution.py:398
  174.6 16.6 %shard_map.297 = (bf16[384,1024]{1,0:T(8,128)(2,1)}, f32[6,64,64]{2,1,0:T(8,128)}, f32[768,1024]{1,0:T(8,128)}, f32[384,1024]{1,0:T(8,128)}) custom-call(bf16[1536,1024]{1,0:T(8,128)(2,1)} %get-tuple-element.58.pq_ref, bf16[1536,1024]{1,0:T(8,128)(2,1)} %get-tuple-element.59.pk_ref, bf16[2304,1024]{1,0:T(8,128)(2,1)} %get-tuple-element.60.v_ref.q_ref.k_ref, ...), custom_call_target="tpu_custom_call" | custom-call | tf_op jit(solution)/shard_map/pallas_call | solution.py:398
  193.0 14.2 %shard_map.300 = (bf16[2,768,1024]{2,1,0:T(8,128)(2,1)}, f32[12,64,64]{2,1,0:T(8,128)}) custom-call(bf16[1536,1024]{1,0:T(8,128)(2,1)} %get-tuple-element.59.pk_ref, bf16[2304,1024]{1,0:T(8,128)(2,1)} %get-tuple-element.60.v_ref.q_ref.k_ref, bf16[2304,1024]{1,0:T(8,128)(2,1)} %get-tuple-element.60.v_ref.q_ref.k_ref, ...), custom_call_target="tpu_custom_call" | custom-call | tf_op jit(solution)/shard_map/pallas_call | solution.py:398
  209.1 10.0 %shard_map.303 = (f32[16,48,896]{2,1,0:T(8,128)}, f32[8,48,896]{2,1,0:T(8,128)}, f32[8,48,896]{2,1,0:T(8,128)}) custom-call(s32[33]{0:T(128)} %add_add_fusion.1.table_ref, bf16[768,1024]{1,0:T(8,128)(2,1)} %get-tuple-element.83.refs_0_, bf16[2,768,1024]{2,1,0:T(8,128)(2,1)} %get-tuple-element.78.dkv_ref.refs_1_.refs_2_.refs_3_.refs_4_, ...), custom_call_target="tpu_custom_call" | custom-call | tf_op jit(solution)/shard_map/pallas_call | solution.py:540
  220.6 6.2 %shard_map.302 = (f32[16,48,384]{2,1,0:T(8,128)}, f32[8,48,384]{2,1,0:T(8,128)}, f32[8,48,384]{2,1,0:T(8,128)}) custom-call(s32[33]{0:T(128)} %add_add_fusion.table_ref, bf16[768,1024]{1,0:T(8,128)(2,1)} %get-tuple-element.83.refs_0_, bf16[384,1024]{1,0:T(8,128)(2,1)} %get-tuple-element.165.refs_1_, bf16[384,1024]{1,0:T(8,128)(2,1)} %get-tuple-element.164.refs_2_), custom_call_target="tpu_custom_call" | custom-call | tf_op jit(solution)/shard_map/pallas_call | solution.py:540
  235.4 3.6 slice_add_fusion.1
  239.9 3.7 slice_add_fusion
  246.3 10.1 %shard_map.301 = (f32[1024,768]{1,0:T(8,128)}, f32[8,768]{1,0:T(8,128)}) custom-call(bf16[384,1024]{1,0:T(8,128)(2,1)} %get-tuple-element.71.dq0_ref, bf16[384,1024]{1,0:T(8,128)(2,1)} %get-tuple-element.72.dq1_ref, bf16[2,768,1024]{2,1,0:T(8,128)(2,1)} %get-tuple-element.78.dkv_ref.refs_1_.refs_2_.refs_3_.refs_4_, bf16[768,2304]{1,0:T(8,128)(2,1)} %w_ref.3, ...), custom_call_target="tpu_custom_call" | custom-call | tf_op jit(solution)/shard_map/pallas_call | solution.py:398
  257.1 57.9 %collective-permute-done.2 = f32[4,48,384]{2,1,0:T(8,128)S(1)} collective-permute-done((f32[4,48,384]{2,1,0:T(8,128)S(1)}, f32[4,48,384]{2,1,0:T(8,128)S(1)}, u32[]{:S(2)}, u32[]{:S(2)}) %collective-permute-start.2) | collective-permute-done | bytes 294944 | tf_op jit(solution)/shard_map/ppermute | solution.py:553
  317.7 4.6 %all-to-all-start.4 = ((f32[32,1,384]{2,1,0:T(1,128)}), f32[32,1,384]{2,1,0:T(1,128)S(1)}, u32[]{:S(2)}, u32[]{:S(2)}) async-start(f32[32,1,384]{2,1,0:T(1,128)} %all_to_all.22), calls=%async_computation.4 | async-start | bytes 98304 | tf_op jit(solution)/shard_map/all_to_all | solution.py:620
  322.4 7.2 %all-to-all-done.4 = f32[32,1,384]{2,1,0:T(1,128)S(1)} async-done(((f32[32,1,384]{2,1,0:T(1,128)}), f32[32,1,384]{2,1,0:T(1,128)S(1)}, u32[]{:S(2)}, u32[]{:S(2)}) %all-to-all-start.4) | async-done | bytes 49184 | tf_op jit(solution)/shard_map/all_to_all | solution.py:620
  330.6 2.8 fusion.6
  337.8 3.1 collective-permute-done.5
  345.2 4.5 %fusion.4 = (f32[4,192,384]{2,1,0:T(8,128)S(1)}, f32[4,192,384]{2,1,0:T(8,128)}) fusion(f32[16,192,384]{2,1,0:T(8,128)} %collective-permute-done.21, f32[8,192,384]{2,1,0:T(8,128)} %collective-permute-done.22, f32[8,192,384]{2,1,0:T(8,128)} %get-tuple-element.101), kind=kLoop, calls=%fused_computation.13 | loop fusion | flops 1179648 | bytes 9437184 | tf_op jit(solution)/shard_map/add | solution.py:575
  350.4 4.5 %fusion.2 = (f32[4,48,1920]{2,1,0:T(8,128)S(1)}, f32[4,48,1920]{2,1,0:T(8,128)}) fusion(f32[16,48,1920]{2,1,0:T(8,128)} %collective-permute-done.14, f32[8,48,1920]{2,1,0:T(8,128)} %collective-permute-done.15, f32[8,48,1920]{2,1,0:T(8,128)S(1)} %copy-done.2), kind=kLoop, calls=%fused_computation.8 | loop fusion | flops 1474560 | bytes 11796480 | tf_op jit(solution)/shard_map/add | solution.py:575
  358.8 4.0 collective-permute-done.11
  364.5 13.6 %collective-permute-done.12 = f32[1,48,896]{2,1,0:T(8,128)S(1)} collective-permute-done((f32[1,48,896]{2,1,0:T(8,128)S(1)}, f32[1,48,896]{2,1,0:T(8,128)S(1)}, u32[]{:S(2)}, u32[]{:S(2)}) %collective-permute-start.12) | collective-permute-done | bytes 172064 | tf_op jit(solution)/shard_map/ppermute | solution.py:553
  385.2 11.6 %collective-permute-done.24 = f32[2,192,384]{2,1,0:T(8,128)S(1)} collective-permute-done((f32[2,192,384]{2,1,0:T(8,128)S(1)}, f32[2,192,384]{2,1,0:T(8,128)S(1)}, u32[]{:S(2)}, u32[]{:S(2)}) %collective-permute-start.24) | collective-permute-done | bytes 589856 | tf_op jit(solution)/shard_map/ppermute | solution.py:553
  400.6 19.2 %collective-permute-done.25 = f32[1,192,384]{2,1,0:T(8,128)S(1)} collective-permute-done((f32[1,192,384]{2,1,0:T(8,128)S(1)}, f32[1,192,384]{2,1,0:T(8,128)S(1)}, u32[]{:S(2)}, u32[]{:S(2)}) %collective-permute-start.25) | collective-permute-done | bytes 294944 | tf_op jit(solution)/shard_map/ppermute | solution.py:553
  420.5 4.2 collective-permute-done.18
  428.5 6.2 %collective-permute-done.19 = f32[1,48,1920]{2,1,0:T(8,128)} collective-permute-done((f32[1,48,1920]{2,1,0:T(8,128)}, f32[1,48,1920]{2,1,0:T(8,128)}, u32[]{:S(2)}, u32[]{:S(2)}) %collective-permute-start.19) | collective-permute-done | bytes 368672 | tf_op jit(solution)/shard_map/ppermute | solution.py:553
  (180 shorter events, 84.6 us)
Async XLA Ops:
  19.7 23.6 %all-to-all-start = ((f32[32,26,128]{2,1,0:T(8,128)}), f32[32,26,128]{2,1,0:T(8,128)S(1)}, u32[]{:S(2)}, u32[]{:S(2)}) async-start(f32[32,26,128]{2,1,0:T(8,128)} %get-tuple-element.65), calls=%async_computation | async-start | bytes 1048576 | tf_op jit(solution)/shard_map/all_to_all | solution.py:603
  46.0 24.9 %all-to-all-start.1 = ((f32[32,26,128]{2,1,0:T(8,128)}), f32[32,26,128]{2,1,0:T(8,128)S(1)}, u32[]{:S(2)}, u32[]{:S(2)}) async-start(f32[32,26,128]{2,1,0:T(8,128)} %shard_map.295), calls=%async_computation.1 | async-start | bytes 1048576 | tf_op jit(solution)/shard_map/all_to_all | solution.py:609
  127.0 112.9 %collective-permute-start.14 = (f32[16,48,1920]{2,1,0:T(8,128)}, f32[16,48,1920]{2,1,0:T(8,128)}, u32[]{:S(2)}, u32[]{:S(2)}) collective-permute-start(f32[16,48,1920]{2,1,0:T(8,128)} %get-tuple-element.99), channel_id=1, source_target_pairs={{0,8},{1,9},{2,10},{3,11},{4,12},{5,13},{6,14},{7,15},{8,0},{9,1},... | collective-permute-start | bytes 17694728 | tf_op jit(solution)/shard_map/ppermute | solution.py:553
  127.0 22.0 %all-to-all-start.2 = ((f32[32,26,128]{2,1,0:T(8,128)}), f32[32,26,128]{2,1,0:T(8,128)S(1)}, u32[]{:S(2)}, u32[]{:S(2)}) async-start(f32[32,26,128]{2,1,0:T(8,128)} %get-tuple-element.77), calls=%async_computation.2 | async-start | bytes 1048576 | tf_op jit(solution)/shard_map/all_to_all | solution.py:603
  146.0 89.4 %collective-permute-start.21 = (f32[16,192,384]{2,1,0:T(8,128)}, f32[16,192,384]{2,1,0:T(8,128)}, u32[]{:S(2)}, u32[]{:S(2)}) collective-permute-start(f32[16,192,384]{2,1,0:T(8,128)} %get-tuple-element.103), channel_id=1, source_target_pairs={{0,8},{1,9},{2,10},{3,11},{4,12},{5,13},{6,14},{7,15},{8,0},{9,1},... | collective-permute-start | bytes 14155784 | tf_op jit(solution)/shard_map/ppermute | solution.py:553
  151.8 40.4 %all-to-all-start.3 = ((f32[32,26,128]{2,1,0:T(8,128)}), f32[32,26,128]{2,1,0:T(8,128)S(1)}, u32[]{:S(2)}, u32[]{:S(2)}) async-start(f32[32,26,128]{2,1,0:T(8,128)} %shard_map.299), calls=%async_computation.3 | async-start | bytes 1048576 | tf_op jit(solution)/shard_map/all_to_all | solution.py:609
  219.1 13.6 %collective-permute-start.7 = (f32[16,48,896]{2,1,0:T(8,128)}, f32[16,48,896]{2,1,0:T(8,128)S(1)}, u32[]{:S(2)}, u32[]{:S(2)}) collective-permute-start(f32[16,48,896]{2,1,0:T(8,128)} %get-tuple-element.92), channel_id=1, source_target_pairs={{0,8},{1,9},{2,10},{3,11},{4,12},{5,13},{6,14},{7,15},{8,0},{9,1},... | collective-permute-start | bytes 8257544 | tf_op jit(solution)/shard_map/ppermute | solution.py:553
  231.0 13.3 %collective-permute-start.1 = (f32[8,48,384]{2,1,0:T(8,128)S(1)}, f32[8,48,384]{2,1,0:T(8,128)S(1)}, u32[]{:S(2)}, u32[]{:S(2)}) collective-permute-start(f32[8,48,384]{2,1,0:T(8,128)S(1)} %slice_add_fusion.13), channel_id=1, source_target_pairs={{0,2},{1,3},{2,0},{3,1},{4,6},{5,7},{6,4},{7,5},{8,24},{9,25},{10,... | collective-permute-start | bytes 1769480 | tf_op jit(solution)/shard_map/ppermute | solution.py:553
  234.0 96.6 %collective-permute-start.8 = (f32[8,48,896]{2,1,0:T(8,128)}, f32[8,48,896]{2,1,0:T(8,128)}, u32[]{:S(2)}, u32[]{:S(2)}) collective-permute-start(f32[8,48,896]{2,1,0:T(8,128)} %slice_add_fusion.4), channel_id=1, source_target_pairs={{0,16},{1,17},{2,18},{3,19},{4,20},{5,21},{6,22},{7,23},{8,9},{9,8... | collective-permute-start | bytes 4128776 | tf_op jit(solution)/shard_map/ppermute | solution.py:553
  239.0 106.2 %collective-permute-start.22 = (f32[8,192,384]{2,1,0:T(8,128)}, f32[8,192,384]{2,1,0:T(8,128)}, u32[]{:S(2)}, u32[]{:S(2)}) collective-permute-start(f32[8,192,384]{2,1,0:T(8,128)} %slice_add_fusion.1), channel_id=1, source_target_pairs={{0,16},{1,17},{2,18},{3,19},{4,20},{5,21},{6,22},{7,23},{8,9},{9,8... | collective-permute-start | bytes 7077896 | tf_op jit(solution)/shard_map/ppermute | solution.py:553
  243.7 106.8 %collective-permute-start.15 = (f32[8,48,1920]{2,1,0:T(8,128)}, f32[8,48,1920]{2,1,0:T(8,128)}, u32[]{:S(2)}, u32[]{:S(2)}) collective-permute-start(f32[8,48,1920]{2,1,0:T(8,128)} %slice_add_fusion), channel_id=1, source_target_pairs={{0,2},{1,3},{2,0},{3,1},{4,6},{5,7},{6,4},{7,5},{8,24},{9,25},{10,... | collective-permute-start | bytes 8847368 | tf_op jit(solution)/shard_map/ppermute | solution.py:553
  244.3 70.7 %collective-permute-start.2 = (f32[4,48,384]{2,1,0:T(8,128)S(1)}, f32[4,48,384]{2,1,0:T(8,128)S(1)}, u32[]{:S(2)}, u32[]{:S(2)}) collective-permute-start(f32[4,48,384]{2,1,0:T(8,128)S(1)} %get-tuple-element.163), channel_id=1, source_target_pairs={{0,16},{1,17},{2,18},{3,19},{4,20},{5,21},{6,22},{7,23},{8,9},{9,8... | collective-permute-start | bytes 884744 | tf_op jit(solution)/shard_map/ppermute | solution.py:553
  315.1 14.6 %collective-permute-start.3 = (f32[2,48,384]{2,1,0:T(8,128)S(1)}, f32[2,48,384]{2,1,0:T(8,128)S(1)}, u32[]{:S(2)}, u32[]{:S(2)}) collective-permute-start(f32[2,48,384]{2,1,0:T(8,128)S(1)} %get-tuple-element.179), channel_id=1, source_target_pairs={{0,1},{1,0},{2,3},{3,2},{4,5},{5,4},{6,7},{7,6},{8,10},{9,11},{10,... | collective-permute-start | bytes 442376 | tf_op jit(solution)/shard_map/ppermute | solution.py:553
  317.7 11.9 %all-to-all-start.4 = ((f32[32,1,384]{2,1,0:T(1,128)}), f32[32,1,384]{2,1,0:T(1,128)S(1)}, u32[]{:S(2)}, u32[]{:S(2)}) async-start(f32[32,1,384]{2,1,0:T(1,128)} %all_to_all.22), calls=%async_computation.4 | async-start | bytes 98304 | tf_op jit(solution)/shard_map/all_to_all | solution.py:620
  329.7 6.8 %collective-permute-start.4 = (f32[1,48,384]{2,1,0:T(8,128)S(1)}, f32[1,48,384]{2,1,0:T(8,128)S(1)}, u32[]{:S(2)}, u32[]{:S(2)}) collective-permute-start(f32[1,48,384]{2,1,0:T(8,128)S(1)} %slice_add_fusion.26), channel_id=1, source_target_pairs={{0,4},{1,5},{2,6},{3,7},{4,0},{5,1},{6,2},{7,3},{8,12},{9,13},{10,... | collective-permute-start | bytes 221192 | tf_op jit(solution)/shard_map/ppermute | solution.py:553
  333.4 11.1 %collective-permute-start.9 = (f32[4,48,896]{2,1,0:T(8,128)}, f32[4,48,896]{2,1,0:T(8,128)S(1)}, u32[]{:S(2)}, u32[]{:S(2)}) collective-permute-start(f32[4,48,896]{2,1,0:T(8,128)} %get-tuple-element.157), channel_id=1, source_target_pairs={{0,1},{1,0},{2,3},{3,2},{4,5},{5,4},{6,7},{7,6},{8,10},{9,11},{10,... | collective-permute-start | bytes 2064392 | tf_op jit(solution)/shard_map/ppermute | solution.py:553
  336.5 4.4 collective-permute-start.5
  341.8 16.0 %collective-permute-start.6 = (f32[96,384]{0,1:T(8,128)}, f32[96,384]{0,1:T(8,128)S(1)}, u32[]{:S(2)}, u32[]{:S(2)}) collective-permute-start(f32[96,384]{0,1:T(8,128)} %copy.79), channel_id=1, source_target_pairs={{0,8},{1,9},{2,10},{3,11},{4,12},{5,13},{6,14},{7,15},{8,0},{9,1},... | collective-permute-start | bytes 442376 | tf_op jit(solution)/shard_map/ppermute | solution.py:553
  344.6 10.8 %collective-permute-start.10 = (f32[2,48,896]{2,1,0:T(8,128)S(1)}, f32[2,48,896]{2,1,0:T(8,128)S(1)}, u32[]{:S(2)}, u32[]{:S(2)}) collective-permute-start(f32[2,48,896]{2,1,0:T(8,128)S(1)} %get-tuple-element.169), channel_id=1, source_target_pairs={{0,2},{1,3},{2,0},{3,1},{4,6},{5,7},{6,4},{7,5},{8,24},{9,25},{10,... | collective-permute-start | bytes 1032200 | tf_op jit(solution)/shard_map/ppermute | solution.py:553
  349.7 28.8 %collective-permute-start.23 = (f32[4,192,384]{2,1,0:T(8,128)}, f32[4,192,384]{2,1,0:T(8,128)}, u32[]{:S(2)}, u32[]{:S(2)}) collective-permute-start(f32[4,192,384]{2,1,0:T(8,128)} %get-tuple-element.155), channel_id=1, source_target_pairs={{0,1},{1,0},{2,3},{3,2},{4,5},{5,4},{6,7},{7,6},{8,10},{9,11},{10,... | collective-permute-start | bytes 3538952 | tf_op jit(solution)/shard_map/ppermute | solution.py:553
  354.9 26.4 %collective-permute-start.16 = (f32[4,48,1920]{2,1,0:T(8,128)}, f32[4,48,1920]{2,1,0:T(8,128)}, u32[]{:S(2)}, u32[]{:S(2)}) collective-permute-start(f32[4,48,1920]{2,1,0:T(8,128)} %get-tuple-element.153), channel_id=1, source_target_pairs={{0,16},{1,17},{2,18},{3,19},{4,20},{5,21},{6,22},{7,23},{8,9},{9,8... | collective-permute-start | bytes 4423688 | tf_op jit(solution)/shard_map/ppermute | solution.py:553
  355.4 7.3 %collective-permute-start.11 = (f32[1,48,896]{2,1,0:T(8,128)S(1)}, f32[1,48,896]{2,1,0:T(8,128)S(1)}, u32[]{:S(2)}, u32[]{:S(2)}) collective-permute-start(f32[1,48,896]{2,1,0:T(8,128)S(1)} %slice_add_fusion.22), channel_id=1, source_target_pairs={{0,4},{1,5},{2,6},{3,7},{4,0},{5,1},{6,2},{7,3},{8,12},{9,13},{10,... | collective-permute-start | bytes 516104 | tf_op jit(solution)/shard_map/ppermute | solution.py:553
  362.8 15.4 %collective-permute-start.12 = (f32[1,48,896]{2,1,0:T(8,128)S(1)}, f32[1,48,896]{2,1,0:T(8,128)S(1)}, u32[]{:S(2)}, u32[]{:S(2)}) collective-permute-start(f32[1,48,896]{2,1,0:T(8,128)S(1)} %fusion.11), channel_id=1, source_target_pairs={{0,16},{1,17},{2,18},{3,19},{4,20},{5,21},{6,22},{7,23},{8,24},{9,... | collective-permute-start | bytes 516104 | tf_op jit(solution)/shard_map/ppermute | solution.py:553
  378.4 5.9 %collective-permute-start.13 = (f32[96,896]{0,1:T(8,128)S(1)}, f32[96,896]{0,1:T(8,128)S(1)}, u32[]{:S(2)}, u32[]{:S(2)}) collective-permute-start(f32[96,896]{0,1:T(8,128)S(1)} %copy.82), channel_id=1, source_target_pairs={{0,8},{1,9},{2,10},{3,11},{4,12},{5,13},{6,14},{7,15},{8,0},{9,1},... | collective-permute-start | bytes 1032200 | tf_op jit(solution)/shard_map/ppermute | solution.py:553
  379.9 16.9 %collective-permute-start.24 = (f32[2,192,384]{2,1,0:T(8,128)S(1)}, f32[2,192,384]{2,1,0:T(8,128)S(1)}, u32[]{:S(2)}, u32[]{:S(2)}) collective-permute-start(f32[2,192,384]{2,1,0:T(8,128)S(1)} %get-tuple-element.161), channel_id=1, source_target_pairs={{0,2},{1,3},{2,0},{3,1},{4,6},{5,7},{6,4},{7,5},{8,24},{9,25},{10,... | collective-permute-start | bytes 1769480 | tf_op jit(solution)/shard_map/ppermute | solution.py:553
  382.8 15.3 %collective-permute-start.17 = (f32[2,48,1920]{2,1,0:T(8,128)S(1)}, f32[2,48,1920]{2,1,0:T(8,128)S(1)}, u32[]{:S(2)}, u32[]{:S(2)}) collective-permute-start(f32[2,48,1920]{2,1,0:T(8,128)S(1)} %get-tuple-element.159), channel_id=1, source_target_pairs={{0,1},{1,0},{2,3},{3,2},{4,5},{5,4},{6,7},{7,6},{8,10},{9,11},{10,... | collective-permute-start | bytes 2211848 | tf_op jit(solution)/shard_map/ppermute | solution.py:553
  396.9 23.0 %collective-permute-start.25 = (f32[1,192,384]{2,1,0:T(8,128)S(1)}, f32[1,192,384]{2,1,0:T(8,128)S(1)}, u32[]{:S(2)}, u32[]{:S(2)}) collective-permute-start(f32[1,192,384]{2,1,0:T(8,128)S(1)} %slice_add_fusion.18), channel_id=1, source_target_pairs={{0,4},{1,5},{2,6},{3,7},{4,0},{5,1},{6,2},{7,3},{8,12},{9,13},{10,... | collective-permute-start | bytes 884744 | tf_op jit(solution)/shard_map/ppermute | solution.py:553
  398.1 26.6 %collective-permute-start.18 = (f32[1,48,1920]{2,1,0:T(8,128)S(1)}, f32[1,48,1920]{2,1,0:T(8,128)S(1)}, u32[]{:S(2)}, u32[]{:S(2)}) collective-permute-start(f32[1,48,1920]{2,1,0:T(8,128)S(1)} %slice_add_fusion.14), channel_id=1, source_target_pairs={{0,4},{1,5},{2,6},{3,7},{4,0},{5,1},{6,2},{7,3},{8,12},{9,13},{10,... | collective-permute-start | bytes 1105928 | tf_op jit(solution)/shard_map/ppermute | solution.py:553
  419.9 8.1 %collective-permute-start.26 = (f32[1,192,384]{2,1,0:T(8,128)S(1)}, f32[1,192,384]{2,1,0:T(8,128)S(1)}, u32[]{:S(2)}, u32[]{:S(2)}) collective-permute-start(f32[1,192,384]{2,1,0:T(8,128)S(1)} %fusion.8), channel_id=1, source_target_pairs={{0,16},{1,17},{2,18},{3,19},{4,20},{5,21},{6,22},{7,23},{8,24},{9,... | collective-permute-start | bytes 884744 | tf_op jit(solution)/shard_map/ppermute | solution.py:553
  425.5 9.2 %collective-permute-start.19 = (f32[1,48,1920]{2,1,0:T(8,128)}, f32[1,48,1920]{2,1,0:T(8,128)}, u32[]{:S(2)}, u32[]{:S(2)}) collective-permute-start(f32[1,48,1920]{2,1,0:T(8,128)} %fusion.7), channel_id=1, source_target_pairs={{0,16},{1,17},{2,18},{3,19},{4,20},{5,21},{6,22},{7,23},{8,24},{9,... | collective-permute-start | bytes 1105928 | tf_op jit(solution)/shard_map/ppermute | solution.py:553
  428.4 10.2 %collective-permute-start.27 = (f32[384,384]{0,1:T(8,128)S(1)}, f32[384,384]{0,1:T(8,128)}, u32[]{:S(2)}, u32[]{:S(2)}) collective-permute-start(f32[384,384]{0,1:T(8,128)S(1)} %copy.85), channel_id=1, source_target_pairs={{0,8},{1,9},{2,10},{3,11},{4,12},{5,13},{6,14},{7,15},{8,0},{9,1},... | collective-permute-start | bytes 1769480 | tf_op jit(solution)/shard_map/ppermute | solution.py:553
  435.9 4.9 %collective-permute-start.20 = (f32[96,1920]{1,0:T(8,128)S(1)}, f32[96,1920]{1,0:T(8,128)}, u32[]{:S(2)}, u32[]{:S(2)}) collective-permute-start(f32[96,1920]{1,0:T(8,128)S(1)} %bitcast.24), channel_id=1, source_target_pairs={{0,8},{1,9},{2,10},{3,11},{4,12},{5,13},{6,14},{7,15},{8,0},{9,1},... | collective-permute-start | bytes 2211848 | tf_op jit(solution)/shard_map/ppermute | solution.py:553
  (25 other events, 180.1 us)
